TPU v7x, 32 devices: a whole 2x2x4 slice. The times are simulated.
32 devices in a mesh: dp: 16 (over z, x, core), tensor: 2 (over y).
Axes of the slice: x: 2, y: 2, z: 4, core: 2. Of those that a mesh axis runs over, the one named last changes fastest.
Arguments:
- tokens: bfloat16 [32768, 768], P(('dp', 'tensor')), may hold values from -6 to 6
- segment_ids: int32 [16, 2048], P('dp'), may hold values from 0 to 15, never falling along the last dimension, each value on 1 to 1024 neighbouring positions
- ln1_gain: bfloat16 [768], P('dp'), may hold values from 0.25 to 1.75
- ln1_bias: bfloat16 [768], P('dp'), may hold values from -1.796875 to 1.796875
- w_qkv: bfloat16 [768, 3, 768], P('dp', None, 'tensor'), may hold values from -0.3125 to 0.3125
- b_qv: bfloat16 [2, 768], P(None, 'dp'), may hold values from -1.796875 to 1.796875
- w_attn_out: bfloat16 [768, 768], P('tensor', 'dp'), may hold values from -3 to 3
- b_attn_out: bfloat16 [768], P('dp'), may hold values from -6 to 6
- ln2_gain: bfloat16 [768], P('dp'), may hold values from 0.25 to 1.75
- ln2_bias: bfloat16 [768], P('dp'), may hold values from -1.796875 to 1.796875
- w_fc: bfloat16 [768, 3072], P('dp', 'tensor'), may hold values from -0.21875 to 0.21875
- b_fc: bfloat16 [3072], P('dp'), may hold values from -1.796875 to 1.796875
- w_proj: bfloat16 [3072, 768], P('tensor', 'dp'), may hold values from -0.8984375 to 0.8984375
- b_proj: bfloat16 [768], P('dp'), may hold values from -6 to 6
- cotangent: bfloat16 [32768, 768], P(('dp', 'tensor')), may hold values from -6 to 6
Outputs:
- block_out: bfloat16 [32768, 768], P(('dp', 'tensor'))
- grad_tokens: bfloat16 [32768, 768], P(('dp', 'tensor'))
- grad_ln1_gain: float32 [768], P('dp')
- grad_ln1_bias: float32 [768], P('dp')
- grad_w_qkv: float32 [768, 3, 768], P('dp', None, 'tensor')
- grad_b_qv: float32 [2, 768], P(None, 'dp')
- grad_w_attn_out: float32 [768, 768], P('tensor', 'dp')
- grad_b_attn_out: float32 [768], P('dp')
- grad_ln2_gain: float32 [768], P('dp')
- grad_ln2_bias: float32 [768], P('dp')
- grad_w_fc: float32 [768, 3072], P('dp', 'tensor')
- grad_b_fc: float32 [3072], P('dp')
- grad_w_proj: float32 [3072, 768], P('tensor', 'dp')
- grad_b_proj: float32 [768], P('dp')
Inputs may be any that keep to these rules, and one draw needn't show every extreme that they name: `segment_ids`: in each sequence the document numbers never fall; each document has 1 to 1024 tokens, and one has exactly 1024.
All inputs are finite; a program needn't handle non-finite values.
Results may differ from a plain program's by a relative error of at most 0.02.
Values may be sent and summed in bfloat16 or wider, within the bound.
A program may use at most 256 MiB of HBM per device.

v0:
```python
import jax
import jax.numpy as jnp
from jax import lax
from jax.sharding import PartitionSpec as P

HEAD_DIM = 64


EPSILON = 1e-05
BRANCH_SCALE = 48.0 ** (-0.5)
MASKED_SCORE = -1e30


def layer_norm(values, gain, offsets):
    centered = values - jnp.mean(values, axis=-1, keepdims=True)
    variance = jnp.mean(centered * centered, axis=-1, keepdims=True)
    return centered * lax.rsqrt(variance + EPSILON) * gain + offsets


def gelu_tanh(values):
    return jax.nn.gelu(values, approximate=True)


def contract_rows(left, right):
    return lax.dot_general(
        left, right, (((0,), (0,)), ((), ())), preferred_element_type=jnp.float32
    )


def contract_cols(left, right):
    return lax.dot_general(
        left, right, (((1,), (1,)), ((), ())), preferred_element_type=jnp.float32
    )


def visible_mask(seg_row, row_start, block_rows):
    seq_len = seg_row.shape[0]
    seg_query = lax.dynamic_slice_in_dim(seg_row, row_start, block_rows, 0)
    query_pos = row_start + jnp.arange(block_rows, dtype=jnp.int32)
    key_pos = jnp.arange(seq_len, dtype=jnp.int32)
    return (seg_query[:, None] == seg_row[None, :]) & (query_pos[:, None] >= key_pos[None, :])


def on_device(
    tokens,
    segment_ids,
    ln1_gain,
    ln1_bias,
    w_qkv,
    b_qv,
    w_attn_out,
    b_attn_out,
    ln2_gain,
    ln2_bias,
    w_fc,
    b_fc,
    w_proj,
    b_proj,
    cotangent,
):
    model_width = tokens.shape[1]
    local_rows = tokens.shape[0]
    local_cols = w_qkv.shape[2]
    hidden_cols = w_fc.shape[1]
    heads_here = local_cols // HEAD_DIM
    seg_row = segment_ids[0]
    seq_len = seg_row.shape[0]
    score_scale = HEAD_DIM ** (-0.5)
    tensor_pos = lax.axis_index("tensor")
    gain_attn, offset_attn, qkv_weight, qv_bias_all, out_weight, out_bias = (
        lax.all_gather(ln1_gain, "dp", axis=0, tiled=True),
        lax.all_gather(ln1_bias, "dp", axis=0, tiled=True),
        lax.all_gather(w_qkv, "dp", axis=0, tiled=True),
        lax.all_gather(b_qv, "dp", axis=1, tiled=True),
        lax.all_gather(w_attn_out, "dp", axis=1, tiled=True),
        lax.all_gather(b_attn_out, "dp", axis=0, tiled=True),
    )
    qkv_flat_weight = qkv_weight.reshape(model_width, 3 * local_cols)
    qv_bias = lax.dynamic_slice_in_dim(qv_bias_all, tensor_pos * local_cols, local_cols, 1).astype(
        jnp.float32
    )
    qkv_bias = jnp.stack([qv_bias[0], jnp.zeros((local_cols,), jnp.float32), qv_bias[1]])
    residual_in = tokens.astype(jnp.float32)
    normed_one = layer_norm(
        residual_in, gain_attn.astype(jnp.float32), offset_attn.astype(jnp.float32)
    ).astype(jnp.bfloat16)
    full_one = lax.all_gather(normed_one, "tensor", axis=0, tiled=True)
    projected = (
        jnp.dot(full_one, qkv_flat_weight, preferred_element_type=jnp.float32).reshape(
            seq_len, 3, local_cols
        )
        + qkv_bias
    ).astype(jnp.bfloat16)
    queries = projected[:, 0]
    keys_all = projected[:, 1]
    values_all = projected[:, 2]
    block_rows = min(512, seq_len)
    starts = jnp.arange(seq_len // block_rows, dtype=jnp.int32) * block_rows

    def forward_block(row_start):
        visible = visible_mask(seg_row, row_start, block_rows)
        query_block = lax.dynamic_slice_in_dim(queries, row_start, block_rows, 0)
        pieces = []
        logsums = []
        for head_index in range(heads_here):
            low_col = head_index * HEAD_DIM
            high_col = low_col + HEAD_DIM
            raw_scores = contract_cols(
                query_block[:, low_col:high_col], keys_all[:, low_col:high_col]
            )
            scores = jnp.where(visible, raw_scores * score_scale, MASKED_SCORE)
            row_max = jnp.max(scores, axis=1, keepdims=True)
            exponent = jnp.exp(scores - row_max)
            row_total = jnp.sum(exponent, axis=1, keepdims=True)
            soft_weights = (exponent / row_total).astype(jnp.bfloat16)
            pieces.append(
                jnp.dot(
                    soft_weights,
                    values_all[:, low_col:high_col],
                    preferred_element_type=jnp.float32,
                )
            )
            logsums.append(row_max[:, 0] + jnp.log(row_total[:, 0]))
        return (jnp.concatenate(pieces, axis=1).astype(jnp.bfloat16), jnp.stack(logsums))

    attn_blocks, logsum_blocks = lax.map(forward_block, starts)
    attended = attn_blocks.reshape(seq_len, local_cols)
    attn_branch = lax.psum_scatter(
        jnp.dot(
            lax.slice_in_dim(attended, 0, lax.axis_size("tensor") * local_rows, axis=0),
            out_weight,
            preferred_element_type=jnp.float32,
        ).astype(jnp.bfloat16),
        "tensor",
        scatter_dimension=0,
        tiled=True,
    ).astype(jnp.float32) + out_bias.astype(jnp.float32)
    middle = residual_in + BRANCH_SCALE * attn_branch
    gain_mlp, offset_mlp, fc_weight, fc_bias_all, proj_weight, proj_bias = (
        lax.all_gather(ln2_gain, "dp", axis=0, tiled=True),
        lax.all_gather(ln2_bias, "dp", axis=0, tiled=True),
        lax.all_gather(w_fc, "dp", axis=0, tiled=True),
        lax.all_gather(b_fc, "dp", axis=0, tiled=True),
        lax.all_gather(w_proj, "dp", axis=1, tiled=True),
        lax.all_gather(b_proj, "dp", axis=0, tiled=True),
    )
    fc_bias = lax.dynamic_slice_in_dim(
        fc_bias_all, tensor_pos * hidden_cols, hidden_cols, 0
    ).astype(jnp.float32)
    normed_two = layer_norm(
        middle, gain_mlp.astype(jnp.float32), offset_mlp.astype(jnp.float32)
    ).astype(jnp.bfloat16)
    full_two = lax.all_gather(normed_two, "tensor", axis=0, tiled=True)
    inputs_rows = lax.slice_in_dim(full_two, 0, lax.axis_size("tensor") * local_rows, axis=0)
    activated = gelu_tanh(
        jnp.dot(inputs_rows, fc_weight, preferred_element_type=jnp.float32) + fc_bias
    ).astype(jnp.bfloat16)
    mlp_branch = lax.psum_scatter(
        jnp.dot(activated, proj_weight, preferred_element_type=jnp.float32).astype(jnp.bfloat16),
        "tensor",
        scatter_dimension=0,
        tiled=True,
    ).astype(jnp.float32) + proj_bias.astype(jnp.float32)
    block_out = (middle + BRANCH_SCALE * mlp_branch).astype(jnp.bfloat16)
    (
        gain_attn,
        offset_attn,
        qkv_weight,
        out_weight,
        gain_mlp,
        offset_mlp,
        fc_weight,
        fc_bias_all,
        proj_weight,
    ) = (
        lax.all_gather(ln1_gain, "dp", axis=0, tiled=True),
        lax.all_gather(ln1_bias, "dp", axis=0, tiled=True),
        lax.all_gather(w_qkv, "dp", axis=0, tiled=True),
        lax.all_gather(w_attn_out, "dp", axis=1, tiled=True),
        lax.all_gather(ln2_gain, "dp", axis=0, tiled=True),
        lax.all_gather(ln2_bias, "dp", axis=0, tiled=True),
        lax.all_gather(w_fc, "dp", axis=0, tiled=True),
        lax.all_gather(b_fc, "dp", axis=0, tiled=True),
        lax.all_gather(w_proj, "dp", axis=1, tiled=True),
    )
    qkv_flat_weight = qkv_weight.reshape(model_width, 3 * local_cols)
    fc_bias = lax.dynamic_slice_in_dim(
        fc_bias_all, tensor_pos * hidden_cols, hidden_cols, 0
    ).astype(jnp.float32)
    grad_out = cotangent.astype(jnp.float32)
    scaled_out = BRANCH_SCALE * grad_out
    d_proj_bias = jnp.sum(scaled_out, axis=0)
    d_mlp_full = lax.all_gather(scaled_out.astype(jnp.bfloat16), "tensor", axis=0, tiled=True)
    mlp_block = min(1024, seq_len)

    def mlp_back_block(row_start):
        inputs_rows = lax.dynamic_slice_in_dim(full_two, row_start, mlp_block, 0)
        grad_rows = lax.dynamic_slice_in_dim(d_mlp_full, row_start, mlp_block, 0)
        pre_act = jnp.dot(inputs_rows, fc_weight, preferred_element_type=jnp.float32) + fc_bias
        activated, gelu_back = jax.vjp(gelu_tanh, pre_act)
        d_act = contract_cols(grad_rows, proj_weight)
        d_pre = gelu_back(d_act)[0]
        return (activated.astype(jnp.bfloat16), d_pre.astype(jnp.bfloat16), jnp.sum(d_pre, axis=0))

    act_blocks, dpre_blocks, dbias_blocks = lax.map(
        mlp_back_block, jnp.arange(seq_len // mlp_block, dtype=jnp.int32) * mlp_block
    )
    act_all = act_blocks.reshape(seq_len, hidden_cols)
    d_pre_all = dpre_blocks.reshape(seq_len, hidden_cols)
    d_fc_bias = jnp.sum(dbias_blocks, axis=0)
    d_proj_w = contract_rows(act_all, d_mlp_full)
    d_fc_w = contract_rows(full_two, d_pre_all)
    grad_w_fc, grad_w_proj = (
        lax.psum_scatter(d_fc_w, "dp", scatter_dimension=0, tiled=True),
        lax.psum_scatter(d_proj_w, "dp", scatter_dimension=1, tiled=True),
    )
    d_normed_two = lax.psum_scatter(
        contract_cols(
            lax.slice_in_dim(d_pre_all, 0, lax.axis_size("tensor") * local_rows, axis=0), fc_weight
        ).astype(jnp.bfloat16),
        "tensor",
        scatter_dimension=0,
        tiled=True,
    ).astype(jnp.float32)
    unused_two, norm_back_two = jax.vjp(
        layer_norm, middle, gain_mlp.astype(jnp.float32), offset_mlp.astype(jnp.float32)
    )
    d_middle_part, d_gain_mlp, d_offset_mlp = norm_back_two(d_normed_two)
    d_middle = grad_out + d_middle_part
    scaled_mid = BRANCH_SCALE * d_middle
    d_out_bias = jnp.sum(scaled_mid, axis=0)
    d_attn_full = lax.all_gather(scaled_mid.astype(jnp.bfloat16), "tensor", axis=0, tiled=True)
    d_out_w = contract_rows(attended, d_attn_full)
    d_attended = contract_cols(d_attn_full, out_weight).astype(jnp.bfloat16)

    def backward_block(carry, inputs):
        d_keys_acc, d_values_acc = carry
        row_start, logsum = inputs
        visible = visible_mask(seg_row, row_start, block_rows)
        query_block = lax.dynamic_slice_in_dim(queries, row_start, block_rows, 0)
        grad_block = lax.dynamic_slice_in_dim(d_attended, row_start, block_rows, 0)
        dq_pieces = []
        dk_pieces = []
        dv_pieces = []
        for head_index in range(heads_here):
            low_col = head_index * HEAD_DIM
            high_col = low_col + HEAD_DIM
            query_head = query_block[:, low_col:high_col]
            key_head = keys_all[:, low_col:high_col]
            grad_head = grad_block[:, low_col:high_col]
            raw_scores = contract_cols(query_head, key_head)
            scores = jnp.where(visible, raw_scores * score_scale, MASKED_SCORE)
            soft_weights = jnp.exp(scores - logsum[head_index][:, None])
            d_soft = contract_cols(grad_head, values_all[:, low_col:high_col])
            d_scores = soft_weights * (
                d_soft - jnp.sum(soft_weights * d_soft, axis=1, keepdims=True)
            )
            d_raw = (d_scores * score_scale).astype(jnp.bfloat16)
            dq_pieces.append(jnp.dot(d_raw, key_head, preferred_element_type=jnp.float32))
            dk_pieces.append(contract_rows(d_raw, query_head))
            dv_pieces.append(contract_rows(soft_weights.astype(jnp.bfloat16), grad_head))
        new_carry = (
            d_keys_acc + jnp.concatenate(dk_pieces, axis=1),
            d_values_acc + jnp.concatenate(dv_pieces, axis=1),
        )
        return (new_carry, jnp.concatenate(dq_pieces, axis=1))

    zero_acc = jnp.zeros((seq_len, local_cols), jnp.float32)
    (d_keys, d_values), dq_blocks = lax.scan(
        backward_block, (zero_acc, zero_acc), (starts, logsum_blocks)
    )
    d_queries = dq_blocks.reshape(seq_len, local_cols)
    d_projected = jnp.stack([d_queries, d_keys, d_values], axis=1).astype(jnp.bfloat16)
    part_sums = jnp.sum(d_projected, axis=0, dtype=jnp.float32)
    d_qv_bias = lax.dynamic_update_slice(
        jnp.zeros((2, model_width), jnp.float32),
        jnp.stack([part_sums[0], part_sums[2]]),
        (0, tensor_pos * local_cols),
    )
    d_flat = d_projected.reshape(seq_len, 3 * local_cols)
    d_qkv_w = contract_rows(full_one, d_flat).reshape(model_width, 3, local_cols)
    d_normed_one = lax.psum_scatter(
        contract_cols(d_flat, qkv_flat_weight).astype(jnp.bfloat16),
        "tensor",
        scatter_dimension=0,
        tiled=True,
    ).astype(jnp.float32)
    unused_one, norm_back_one = jax.vjp(
        layer_norm, residual_in, gain_attn.astype(jnp.float32), offset_attn.astype(jnp.float32)
    )
    d_input_part, d_gain_attn, d_offset_attn = norm_back_one(d_normed_one)
    grad_tokens = (d_middle + d_input_part).astype(jnp.bfloat16)
    d_fc_bias_full = lax.dynamic_update_slice(
        jnp.zeros((fc_bias_all.shape[0],), jnp.float32), d_fc_bias, (tensor_pos * hidden_cols,)
    )
    (
        sum_gain_attn,
        sum_offset_attn,
        sum_qv_bias,
        sum_out_bias,
        sum_gain_mlp,
        sum_offset_mlp,
        sum_fc_bias,
        sum_proj_bias,
    ) = (
        lax.psum(d_gain_attn.astype(jnp.bfloat16), "tensor").astype(jnp.float32),
        lax.psum(d_offset_attn.astype(jnp.bfloat16), "tensor").astype(jnp.float32),
        lax.psum(d_qv_bias.astype(jnp.bfloat16), "tensor").astype(jnp.float32),
        lax.psum(d_out_bias.astype(jnp.bfloat16), "tensor").astype(jnp.float32),
        lax.psum(d_gain_mlp.astype(jnp.bfloat16), "tensor").astype(jnp.float32),
        lax.psum(d_offset_mlp.astype(jnp.bfloat16), "tensor").astype(jnp.float32),
        lax.psum(d_fc_bias_full.astype(jnp.bfloat16), "tensor").astype(jnp.float32),
        lax.psum(d_proj_bias.astype(jnp.bfloat16), "tensor").astype(jnp.float32),
    )
    (
        grad_w_qkv,
        grad_w_attn_out,
        grad_ln1_gain,
        grad_ln1_bias,
        grad_b_qv,
        grad_b_attn_out,
        grad_ln2_gain,
        grad_ln2_bias,
        grad_b_fc,
        grad_b_proj,
    ) = (
        lax.psum_scatter(d_qkv_w, "dp", scatter_dimension=0, tiled=True),
        lax.psum_scatter(d_out_w, "dp", scatter_dimension=1, tiled=True),
        lax.psum_scatter(sum_gain_attn, "dp", scatter_dimension=0, tiled=True),
        lax.psum_scatter(sum_offset_attn, "dp", scatter_dimension=0, tiled=True),
        lax.psum_scatter(sum_qv_bias, "dp", scatter_dimension=1, tiled=True),
        lax.psum_scatter(sum_out_bias, "dp", scatter_dimension=0, tiled=True),
        lax.psum_scatter(sum_gain_mlp, "dp", scatter_dimension=0, tiled=True),
        lax.psum_scatter(sum_offset_mlp, "dp", scatter_dimension=0, tiled=True),
        lax.psum_scatter(sum_fc_bias, "dp", scatter_dimension=0, tiled=True),
        lax.psum_scatter(sum_proj_bias, "dp", scatter_dimension=0, tiled=True),
    )
    return (
        block_out,
        grad_tokens,
        grad_ln1_gain,
        grad_ln1_bias,
        grad_w_qkv,
        grad_b_qv,
        grad_w_attn_out,
        grad_b_attn_out,
        grad_ln2_gain,
        grad_ln2_bias,
        grad_w_fc,
        grad_b_fc,
        grad_w_proj,
        grad_b_proj,
    )


def solution(mesh):
    in_specs = (
        P(("dp", "tensor"), None),
        P("dp", None),
        P("dp"),
        P("dp"),
        P("dp", None, "tensor"),
        P(None, "dp"),
        P("tensor", "dp"),
        P("dp"),
        P("dp"),
        P("dp"),
        P("dp", "tensor"),
        P("dp"),
        P("tensor", "dp"),
        P("dp"),
        P(("dp", "tensor"), None),
    )
    out_specs = (
        P(("dp", "tensor"), None),
        P(("dp", "tensor"), None),
        P("dp"),
        P("dp"),
        P("dp", None, "tensor"),
        P(None, "dp"),
        P("tensor", "dp"),
        P("dp"),
        P("dp"),
        P("dp"),
        P("dp", "tensor"),
        P("dp"),
        P("tensor", "dp"),
        P("dp"),
    )
    return jax.shard_map(
        on_device, mesh=mesh, in_specs=in_specs, out_specs=out_specs, check_vma=False
    )
```

profile of v0, /device:TPU:0, one launch (start us, length us, event | category | flops | bytes accessed | tf_op | source)
XLA Modules:
  0.0 1494.2 jit_solution(269349831955712147)
XLA Ops:
  16.5 63.2 %all-reduce.15 = (bf16[768]{0:T(1024)(128)(2,1)}, bf16[768]{0:T(1024)(128)(2,1)}, bf16[768]{0:T(1024)(128)(2,1)}, bf16[768]{0:T(1024)(128)(2,1)S(1)}, bf16[768]{...) all-reduce(bf16[768]{0:T(1024)(128)(2,1)S(1)} %dynamic-update-slice, ...), channel_id=1, replica_groups=mesh['dp'=16,'tensor'=2] {'dp'}, use_global_device_ids=true, to_apply=%add.4 | all-reduce | flops 7680 | bytes 30720
  86.6 17.0 %all-gather = bf16[16,48,2]{1,2,0:T(2,128)(2,1)S(1)} all-gather(bf16[1,48,2]{1,2,0:T(2,128)(2,1)S(1)} %bitcast.226), channel_id=1, replica_groups=mesh['dp'=16,'tensor'=2] {'dp'}, dimensions={0}, use_global_device_ids=true | all-gather | bytes 3264 | tf_op jit(solution)/shard_map/all_gather | solution.py:74
  104.4 22.1 %all_gather.60 = bf16[384,768]{0,1:T(8,128)(2,1)} all-gather(bf16[384,48]{0,1:T(8,128)(2,1)S(1)} %copy-done.41), channel_id=1, replica_groups=mesh['dp'=16,'tensor'=2] {'dp'}, dimensions={1}, use_global_device_ids=true | all-gather | bytes 626688 | tf_op jit(solution)/shard_map/all_gather | solution.py:75
  129.1 7.4 add_convert_fusion
  138.2 145.9 %while.43 = (s32[]{:T(128)}, bf16[4,512,384]{2,1,0:T(8,128)(2,1)}, f32[4,6,512]{2,1,0:T(8,128)}, s32[4]{0:T(128)}, s32[2048]{0:T(1024)}, /*index=5*/s32[1,2048]{...) while((s32[]{:T(128)}, bf16[4,512,384]{2,1,0:T(8,128)(2,1)}, ...), condition=%wide.region_15.16_spmd, body=%wide.region_2.15_spmd.sunk | while | flops 1680012800 | bytes 86346096 | solution.py:126
  293.8 39.7 %reduce-scatter.12.cloned.1.call-done = bf16[1024,768]{1,0:T(8,128)(2,1)} async-done(((bf16[2048,768]{1,0:T(8,128)(2,1)}), bf16[1024,768]{1,0:T(8,128)(2,1)}) %reduce-scatter.12.cloned.1.call-update) | async-done | bytes 1572880 | tf_op jit(solution)/shard_map/reduce_scatter | solution.py:128
  340.2 38.0 %all-gather.17.cloned.1.call-done = bf16[1536,768]{0,1:T(8,128)(2,1)} async-done(((bf16[1536,48]{0,1:T(8,128)(2,1)}), bf16[1536,768]{0,1:T(8,128)(2,1)}) %all-gather.17.cloned.1.call-update) | async-done | bytes 2359312 | tf_op jit(solution)/shard_map/all_gather | solution.py:144
  381.0 42.4 %all-gather.19.cloned.1.call-done = bf16[2048,768]{1,0:T(8,128)(2,1)} async-done(((bf16[1024,768]{1,0:T(8,128)(2,1)}), bf16[2048,768]{1,0:T(8,128)(2,1)}) %all-gather.19.cloned.1.call-update) | async-done | bytes 3145744 | tf_op jit(solution)/shard_map/all_gather | solution.py:193
  423.4 44.7 %all-gather.15.cloned.1.call-done = bf16[768,1536]{1,0:T(8,128)(2,1)} async-done(((bf16[48,1536]{1,0:T(8,128)(2,1)}), bf16[768,1536]{1,0:T(8,128)(2,1)}) %all-gather.15.cloned.1.call-update) | async-done | bytes 2359312 | tf_op jit(solution)/shard_map/all_gather | solution.py:142
  468.2 45.9 %all-gather.13.cloned.1.call-done = bf16[2048,768]{1,0:T(8,128)(2,1)} async-done(((bf16[1024,768]{1,0:T(8,128)(2,1)}), bf16[2048,768]{1,0:T(8,128)(2,1)}) %all-gather.13.cloned.1.call-update) | async-done | bytes 3145744 | tf_op jit(solution)/shard_map/all_gather | solution.py:153
  514.1 47.8 %while.44 = (s32[]{:T(128)}, bf16[2,1024,1536]{2,1,0:T(8,128)(2,1)}, bf16[2,1024,1536]{2,1,0:T(8,128)(2,1)}, f32[2,1536]{1,0:T(2,128)S(1)}, s32[2]{0:T(128)S(1)}...) while((s32[]{:T(128)}, ...), condition=%wide.region_22.23_spmd, body=%wide.region_20.22_spmd.sunk | while | flops 4882168320 | bytes 102281512 | solution.py:205
  516.6 7.7 bitcast_dynamic-update-slice_fusion.7
  524.4 7.8 bitcast_dynamic-update-slice_fusion.8
  540.6 7.7 bitcast_dynamic-update-slice_fusion.7
  548.3 7.8 bitcast_dynamic-update-slice_fusion.8
  562.0 9.1 convolution_convert_fusion.1
  572.7 14.0 convolution_convert_fusion.2
  586.8 27.8 %reduce-scatter.16.cloned.1.call-done = bf16[1024,768]{1,0:T(8,128)(2,1)} async-done(((bf16[2048,768]{1,0:T(8,128)(2,1)}), bf16[1024,768]{1,0:T(8,128)(2,1)}) %reduce-scatter.16.cloned.1.call-update) | async-done | bytes 1572880 | tf_op jit(solution)/shard_map/reduce_scatter | solution.py:217
  618.6 41.6 %reduce-scatter.14.cloned.1.call-done = bf16[1024,768]{1,0:T(8,128)(2,1)} async-done(((bf16[2048,768]{1,0:T(8,128)(2,1)}), bf16[1024,768]{1,0:T(8,128)(2,1)}) %reduce-scatter.14.cloned.1.call-update) | async-done | bytes 1572880 | tf_op jit(solution)/shard_map/reduce_scatter | solution.py:158
  668.3 45.0 %all-gather.21.cloned.1.call-done = bf16[2048,768]{1,0:T(8,128)(2,1)} async-done(((bf16[1024,768]{1,0:T(8,128)(2,1)}), bf16[2048,768]{1,0:T(8,128)(2,1)}) %all-gather.21.cloned.1.call-update) | async-done | bytes 3145744 | tf_op jit(solution)/shard_map/all_gather | solution.py:232
  718.2 344.7 %while.45 = (s32[]{:T(128)}, f32[2048,384]{0,1:T(8,128)}, f32[2048,384]{0,1:T(8,128)}, bf16[4,512,384]{2,1,0:T(8,128)(2,1)}, s32[4]{0:T(128)}, /*index=5*/s32[20...) while((s32[]{:T(128)}, f32[2048,384]{0,1:T(8,128)}, ...), condition=%wide.region_33.34_spmd.clone, body=%wide.region_26.33_spmd.clone.sunk | while | flops 4111463936 | bytes 254159472 | solution.py:269
  1044.5 7.0 select_add_fusion.3
  1079.4 41.8 %reduce-scatter.18.cloned.1.call-done = bf16[1024,768]{1,0:T(8,128)(2,1)} async-done(((bf16[2048,768]{1,0:T(8,128)(2,1)}), bf16[1024,768]{1,0:T(8,128)(2,1)}) %reduce-scatter.18.cloned.1.call-update) | async-done | bytes 1572880 | tf_op jit(solution)/shard_map/reduce_scatter | solution.py:282
  1130.4 7.1 all-reduce.16
  1138.5 10.1 fusion.173
  1150.5 9.5 fusion.172
  1173.3 8.4 fusion.135
  1183.0 60.1 %all-reduce.14 = (f32[768]{0:T(1024)S(1)}, f32[768]{0:T(1024)S(1)}, f32[768]{0:T(1024)S(1)}, f32[768]{0:T(1024)S(1)}, f32[768]{0:T(1024)S(1)}, /*index=5*/f32[3072]{0:T(1024)S(1)}, f32[768]{0:T(1024)S(1)}) all-reduce(bf16[768]{0:T(1024)(128)(2,1)S(1)} %get-tuple-element.392, ...), channel_id=6, replica_groups=mesh['dp'=16,'tensor'=2] {'dp'}, use_global_device_ids=true, to_apply=%region_39.40.clone | all-reduce | flops 7680 | bytes 46080
  1248.6 26.4 %reduce-scatter.26.cloned.1.call-done = f32[1536,48]{0,1:T(8,128)} async-done(((f32[1536,768]{0,1:T(8,128)}), f32[1536,48]{0,1:T(8,128)}) %reduce-scatter.26.cloned.1.call-update) | async-done | bytes 294928 | tf_op jit(solution)/shard_map/reduce_scatter | solution.py:215
  1275.1 78.9 %reduce-scatter.24.cloned.1.call-done = f32[48,1536]{1,0:T(8,128)} async-done(((f32[768,1536]{1,0:T(8,128)}), f32[48,1536]{1,0:T(8,128)}) %reduce-scatter.24.cloned.1.call-update) | async-done | bytes 294928 | tf_op jit(solution)/shard_map/reduce_scatter | solution.py:214
  1353.9 61.6 %reduce-scatter.22.cloned.1.call-done = f32[384,48]{0,1:T(8,128)} async-done(((f32[384,768]{0,1:T(8,128)}), f32[384,48]{0,1:T(8,128)}) %reduce-scatter.22.cloned.1.call-update) | async-done | bytes 73744 | tf_op jit(solution)/shard_map/reduce_scatter | solution.py:328
  1415.5 71.9 %reduce-scatter.20.cloned.1.call-done = f32[48,3,384]{2,0,1:T(8,128)} async-done(((f32[768,3,384]{2,0,1:T(8,128)}), f32[48,3,384]{2,0,1:T(8,128)}) %reduce-scatter.20.cloned.1.call-update) | async-done | bytes 221200 | tf_op jit(solution)/shard_map/reduce_scatter | solution.py:327
  (563 shorter events, 575.9 us)
Async XLA Ops:
  7.2 77.5 %copy-start = (bf16[1024,768]{1,0:T(8,128)(2,1)S(1)}, bf16[1024,768]{1,0:T(8,128)(2,1)}, u32[]{:S(2)}) copy-start(bf16[1024,768]{1,0:T(8,128)(2,1)} %param.21) | copy-start | bytes 4718596
  7.2 119.3 %all-gather.11.cloned.1.call-start = ((), (), s32[]{:S(2)}) async-start(), calls=%async_computation.10 | async-start | bytes 1880064 | tf_op jit(solution)/shard_map/all_gather | solution.py:73
  7.9 121.2 %all-gather.9.cloned.1.call-start = ((), (), s32[]{:S(2)}) async-start(), calls=%async_computation.9 | async-start | bytes 4718592 | tf_op jit(solution)/shard_map/all_gather | solution.py:87
  86.5 246.9 %reduce-scatter.12.cloned.1.call-start = ((), (), s32[]{:S(2)}) async-start(), calls=%async_computation.11 | async-start | bytes 4718592 | tf_op jit(solution)/shard_map/reduce_scatter | solution.py:128
  290.3 43.2 %copy-start.1 = (bf16[1024,768]{1,0:T(8,128)(2,1)S(1)}, bf16[1024,768]{1,0:T(8,128)(2,1)}, u32[]{:S(2)}) copy-start(bf16[1024,768]{1,0:T(8,128)(2,1)} %param.21) | copy-start | bytes 4718596
  290.3 87.9 %all-gather.17.cloned.1.call-start = ((), (), s32[]{:S(2)}) async-start(), calls=%async_computation.14 | async-start | bytes 2506752 | tf_op jit(solution)/shard_map/all_gather | solution.py:144
  290.9 132.5 %all-gather.19.cloned.1.call-start = ((), (), s32[]{:S(2)}) async-start(), calls=%async_computation.16 | async-start | bytes 4718592 | tf_op jit(solution)/shard_map/all_gather | solution.py:193
  293.1 175.1 %all-gather.15.cloned.1.call-start = ((), (), s32[]{:S(2)}) async-start(), calls=%async_computation.13 | async-start | bytes 2506752 | tf_op jit(solution)/shard_map/all_gather | solution.py:142
  293.7 220.4 %all-gather.13.cloned.1.call-start = ((), (), s32[]{:S(2)}) async-start(), calls=%async_computation.12 | async-start | bytes 4718592 | tf_op jit(solution)/shard_map/all_gather | solution.py:153
  293.7 43.5 %copy-start.23 = (f32[768]{0:T(1024)}, f32[768]{0:T(1024)S(1)}, u32[]{:S(2)}) copy-start(f32[768]{0:T(1024)S(1)} %convert_element_type.220) | copy-start | bytes 9220
  293.8 43.5 %copy-start.31 = (f32[768]{0:T(1024)}, f32[768]{0:T(1024)S(1)}, u32[]{:S(2)}) copy-start(f32[768]{0:T(1024)S(1)} %convert_element_type.221) | copy-start | bytes 9220
  340.0 274.6 %reduce-scatter.16.cloned.1.call-start = ((), (), s32[]{:S(2)}) async-start(), calls=%async_computation.17 | async-start | bytes 4718592 | tf_op jit(solution)/shard_map/reduce_scatter | solution.py:217
  571.1 89.1 %reduce-scatter.14.cloned.1.call-start = ((), (), s32[]{:S(2)}) async-start(), calls=%async_computation.15 | async-start | bytes 4718592 | tf_op jit(solution)/shard_map/reduce_scatter | solution.py:158
  572.7 41.9 %copy-start.32 = (f32[768]{0:T(1024)S(1)}, f32[768]{0:T(1024)}, u32[]{:S(2)}) copy-start(f32[768]{0:T(1024)} %copy-done.31) | copy-start | bytes 9220
  572.7 41.9 %copy-start.34 = (f32[1024]{0:T(1024)S(1)}, f32[1024]{0:T(1024)}, u32[]{:S(2)}) copy-start(f32[1024]{0:T(1024)} %copy-done.33) | copy-start | bytes 12292
  586.7 27.9 %copy-start.24 = (f32[768]{0:T(1024)S(1)}, f32[768]{0:T(1024)}, u32[]{:S(2)}) copy-start(f32[768]{0:T(1024)} %copy-done.23) | copy-start | bytes 9220
  586.7 27.9 %copy-start.28 = (f32[1024]{0:T(1024)S(1)}, f32[1024]{0:T(1024)}, u32[]{:S(2)}) copy-start(f32[1024]{0:T(1024)} %copy-done.27) | copy-start | bytes 12292
  586.7 31.8 %copy-start.40 = (f32[1024]{0:T(1024)S(1)}, f32[1024]{0:T(1024)}, u32[]{:S(2)}) copy-start(f32[1024]{0:T(1024)} %copy-done.39) | copy-start | bytes 12292
  586.8 126.5 %all-gather.21.cloned.1.call-start = ((), (), s32[]{:S(2)}) async-start(), calls=%async_computation.18 | async-start | bytes 4718592 | tf_op jit(solution)/shard_map/all_gather | solution.py:232
  668.2 453.0 %reduce-scatter.18.cloned.1.call-start = ((), (), s32[]{:S(2)}) async-start(), calls=%async_computation.19 | async-start | bytes 4718592 | tf_op jit(solution)/shard_map/reduce_scatter | solution.py:282
  668.2 50.0 %copy-start.5 = (bf16[2048,384]{1,0:T(8,128)(2,1)S(1)}, bf16[2048,384]{1,0:T(8,128)(2,1)}, u32[]{:S(2)}) copy-start(bf16[2048,384]{1,0:T(8,128)(2,1)} %copy-done.4) | copy-start | bytes 4718596
  668.2 50.0 %copy-start.7 = (bf16[2048,384]{1,0:T(8,128)(2,1)S(1)}, bf16[2048,384]{1,0:T(8,128)(2,1)}, u32[]{:S(2)}) copy-start(bf16[2048,384]{1,0:T(8,128)(2,1)} %copy-done.6) | copy-start | bytes 4718596
  1077.7 43.5 %copy-start.3 = (bf16[1024,768]{1,0:T(8,128)(2,1)S(1)}, bf16[1024,768]{1,0:T(8,128)(2,1)}, u32[]{:S(2)}) copy-start(bf16[1024,768]{1,0:T(8,128)(2,1)} %param.21) | copy-start | bytes 4718596
  1077.7 43.5 %copy-start.22 = (f32[1024]{0:T(1024)S(1)}, f32[1024]{0:T(1024)}, u32[]{:S(2)}) copy-start(f32[1024]{0:T(1024)} %copy-done.21) | copy-start | bytes 12292
  1077.7 43.5 %copy-start.26 = (f32[768]{0:T(1024)S(1)}, f32[768]{0:T(1024)}, u32[]{:S(2)}) copy-start(f32[768]{0:T(1024)} %copy-done.25) | copy-start | bytes 9220
  1077.7 45.9 %copy-start.38 = (f32[1024]{0:T(1024)S(1)}, f32[1024]{0:T(1024)}, u32[]{:S(2)}) copy-start(f32[1024]{0:T(1024)} %copy-done.37) | copy-start | bytes 12292
  1077.7 45.9 %copy-start.30 = (f32[1024]{0:T(1024)S(1)}, f32[1024]{0:T(1024)}, u32[]{:S(2)}) copy-start(f32[1024]{0:T(1024)} %copy-done.29) | copy-start | bytes 12292
  1077.7 169.5 %reduce-scatter.28.cloned.1.call-start = ((), (), s32[]{:S(2)}) async-start(), calls=%async_computation.24 | async-start | bytes 417792
  1138.5 136.6 %reduce-scatter.26.cloned.1.call-start = ((), (), s32[]{:S(2)}) async-start(), calls=%async_computation.23 | async-start | bytes 5013504 | tf_op jit(solution)/shard_map/reduce_scatter | solution.py:215
  1148.6 205.3 %reduce-scatter.24.cloned.1.call-start = ((), (), s32[]{:S(2)}) async-start(), calls=%async_computation.22 | async-start | bytes 5013504 | tf_op jit(solution)/shard_map/reduce_scatter | solution.py:214
  1160.0 255.5 %reduce-scatter.22.cloned.1.call-start = ((), (), s32[]{:S(2)}) async-start(), calls=%async_computation.21 | async-start | bytes 1253376 | tf_op jit(solution)/shard_map/reduce_scatter | solution.py:328
  1166.3 321.1 %reduce-scatter.20.cloned.1.call-start = ((), (), s32[]{:S(2)}) async-start(), calls=%async_computation.20 | async-start | bytes 3760128 | tf_op jit(solution)/shard_map/reduce_scatter | solution.py:327
  (53 other events, 246.3 us)
Sparse Core Ops, SparseCore 0:
  10.3 43.2 all-gather.10
  86.6 42.1 all-gather.8
  290.4 43.0 reduce-scatter.11
  335.8 42.3 all-gather.16
  379.7 43.7 all-gather.18
  425.8 42.3 all-gather.14
  470.3 43.7 all-gather.12
  571.2 43.3 reduce-scatter.15
  616.8 43.3 reduce-scatter.13
  668.3 44.9 all-gather.20
  1077.8 43.3 reduce-scatter.17
  1138.6 56.7 reduce-scatter.27
  1200.3 74.7 reduce-scatter.25
  1279.4 74.5 reduce-scatter.23
  1358.4 57.0 reduce-scatter.21
  1420.3 67.0 reduce-scatter.19
where the time goes:
time: 1500 us; the launch traced here: 1490 us
  waiting for transfers between devices  608 us (41%)
  matrix products  437 us (29%)
  blocking collectives  169 us (11%)
  other arithmetic  126 us (8%)
  local copies, waits for them, and re-layouts  107 us (7%)
  loops' own time  29.1 us (2%)
  between operations  17.5 us (1%)
    dot_general x77, matrix products, contract_cols(): lax.dot_general(left, right, (((1,), (1,)), ((), ())), preferred_element_...  205 us
    dot_general x52, matrix products, contract_rows(): lax.dot_general(left, right, (((0,), (0,)), ((), ())), preferred_element_...  126 us
    unnamed x2, blocking collectives  123 us
    reduce_scatter x1, waiting for transfers between devices, on_device(): lax.psum_scatter(d_fc_w, 'dp', scatter_dimension=0, tiled=True)  78.9 us
    reduce_scatter x1, waiting for transfers between devices, on_device(): lax.psum_scatter(d_qkv_w, 'dp', scatter_dimension=0, tiled=True)  71.9 us
    reduce_scatter x1, waiting for transfers between devices, on_device(): lax.psum_scatter(d_out_w, 'dp', scatter_dimension=1, tiled=True)  61.6 us
    all_gather x1, waiting for transfers between devices, on_device(): full_two = lax.all_gather(normed_two, 'tensor', axis=0, tiled=True)  45.9 us
    all_gather x1, waiting for transfers between devices, on_device(): lax.all_gather(scaled_mid.astype(jnp.bfloat16), 'tensor', axis=0, tiled=T...  45 us
  transfers between devices with their start and end apart: 16, of which 13 were waited for; matrix products, arithmetic and copies ran while one was open for 6% of the time, Pallas kernels for 0%

commit v1 on v0

v1 whole, which is shorter than its diff:
```python
import functools

import jax
import jax.numpy as jnp
from jax import lax
from jax.experimental import pallas as pl
from jax.experimental.pallas import tpu as pltpu
from jax.sharding import PartitionSpec as P

HD = 64
QB = 256
NEG = -1e30
EPSILON = 1e-05
BRANCH_SCALE = 48.0 ** (-0.5)
SMALL = 128
bf = jnp.bfloat16
f32 = jnp.float32
NT = (((1,), (1,)), ((), ()))
TN = (((0,), (0,)), ((), ()))
BOTH = ("dp", "tensor")


def attn_info(seg, core):
    n=seg.shape[0]; nb=n//QB
    docs=jnp.arange(16,dtype=jnp.int32)
    first=jnp.sum((seg[None,:]<docs[:,None]).astype(jnp.int32),axis=1)
    starts=jnp.sum(jnp.where(seg[None,:]==docs[:,None],first[:,None],0),axis=0)
    blocks=starts.reshape(nb,QB)
    idx=jnp.arange(nb,dtype=jnp.int32)
    low=blocks[:,0]//QB
    mid=jnp.clip((blocks[:,QB-1]+QB-1)//QB,low,idx)
    return starts.reshape(1,n), jnp.concatenate([jnp.reshape(core,(1,)),low,mid]).astype(jnp.int32)

def fwd_kernel(info, own, recv, st_ref, okeep, osend, lse_ref, qm, ks, vt, osc, acc):
    half,cols=own.shape[0],own.shape[1]//3; n=2*half; nb=n//QB; heads=cols//HD; pairs=cols//128
    c=info[0]
    low_lane=(lax.broadcasted_iota(jnp.int32,(1,cols),1)%128)<HD
    zero=jnp.zeros((),bf)
    for base,src in ((c*half,own),((1-c)*half,recv)):
        rows=pl.ds(pl.multiple_of(base,half),half)
        qv=src[:,:cols]*bf(HD**-0.5)
        qm[0,rows]=jnp.where(low_lane,qv,zero)
        qm[1,rows]=jnp.where(low_lane,zero,qv)
        ks[rows]=src[:,cols:2*cols]
        vt[:,rows]=src[:,2*cols:].T
    kio=lax.broadcasted_iota(jnp.int32,(QB,QB),0)
    qio=lax.broadcasted_iota(jnp.int32,(QB,QB),1)
    def qblock(i,_):
        at=pl.multiple_of(i*QB,QB)
        srow=st_ref[:,pl.ds(at,QB)]
        acc[...]=jnp.zeros_like(acc)
        def step(mode,j,carry):
            kat=pl.multiple_of(j*QB,QB)
            if mode:
                mask=kio>=(srow-kat)
                if mode==2: mask=mask&(kio<=qio)
            out=[]
            for h in range(heads):
                m,l=carry[h]
                lanes=slice((h//2)*128,(h//2+1)*128); sub=slice(h*HD,(h+1)*HD)
                s=lax.dot_general(ks[pl.ds(kat,QB),lanes],qm[h%2,pl.ds(at,QB),lanes],NT,preferred_element_type=f32)
                if mode: s=jnp.where(mask,s,NEG)
                mn=jnp.maximum(m,jnp.max(s,axis=0,keepdims=True))
                p=jnp.exp(s-mn); a=jnp.exp(m-mn)
                l=a*l+jnp.sum(p,axis=0,keepdims=True)
                acc[sub]=a*acc[sub]+jnp.dot(vt[sub,pl.ds(kat,QB)],p.astype(bf),preferred_element_type=f32)
                out.append((mn,l))
            return tuple(out)
        one=(jnp.full((1,QB),NEG,f32),jnp.zeros((1,QB),f32))
        carry=step(2,i,(one,)*heads)
        carry=lax.fori_loop(info[1+i],info[1+nb+i],functools.partial(step,1),carry)
        carry=lax.fori_loop(info[1+nb+i],i,functools.partial(step,0),carry)
        for h,(m,l) in enumerate(carry):
            sub=slice(h*HD,(h+1)*HD)
            acc[sub]=acc[sub]/l
            lse_ref[h:h+1,pl.ds(at,QB)]=m+jnp.log(l)
        osc[pl.ds(at,QB)]=acc[...].T.astype(bf)
        return 0
    lax.fori_loop(0,nb,qblock,0)
    okeep[...]=osc[pl.ds(pl.multiple_of(c*half,half),half)]
    osend[...]=osc[pl.ds(pl.multiple_of((1-c)*half,half),half)]

VM=pl.BlockSpec(memory_space=pltpu.VMEM)
SM=pl.BlockSpec(memory_space=pltpu.SMEM)
def attn_fwd(own,recv,starts,info):
    half,cols=own.shape[0],own.shape[1]//3; n=2*half
    return pl.pallas_call(fwd_kernel,
        in_specs=[SM,VM,VM,VM], out_specs=[VM]*3,
        scratch_shapes=[pltpu.VMEM((2,n,cols),bf),pltpu.VMEM((n,cols),bf),pltpu.VMEM((cols,n),bf),pltpu.VMEM((n,cols),bf),pltpu.VMEM((cols,QB),f32)],
        out_shape=[jax.ShapeDtypeStruct((half,cols),bf)]*2+[jax.ShapeDtypeStruct((cols//HD,n),f32)],
        cost_estimate=pl.CostEstimate(flops=2*2*n*n//3*cols,bytes_accessed=8*half*cols*2,transcendentals=n*n*6//3),
        compiler_params=pltpu.CompilerParams(vmem_limit_bytes=48<<20),
    )(info,own,recv,starts)

def bwd_kernel(info, own, recv, doo, dor, oo, orr, st_ref, lse_ref, dkeep, dsend, qm, ks, vs, kt, dom, dlt, dqs, dks, dvs):
    half,cols=own.shape[0],own.shape[1]//3; n=2*half; nb=n//QB; heads=cols//HD; pairs=cols//128
    c=info[0]
    low_lane=(lax.broadcasted_iota(jnp.int32,(1,cols),1)%128)<HD
    zero=jnp.zeros((),bf)
    for base,src,do,o in ((c*half,own,doo,oo),((1-c)*half,recv,dor,orr)):
        rows=pl.ds(pl.multiple_of(base,half),half)
        qv=src[:,:cols]*bf(HD**-0.5)
        qm[0,rows]=jnp.where(low_lane,qv,zero)
        qm[1,rows]=jnp.where(low_lane,zero,qv)
        ks[rows]=src[:,cols:2*cols]
        vs[rows]=src[:,2*cols:]
        kt[:,rows]=src[:,cols:2*cols].T
        dv=do[...]
        dom[0,rows]=jnp.where(low_lane,dv,zero)
        dom[1,rows]=jnp.where(low_lane,zero,dv)
        prod=(dv.astype(f32)*o[...].astype(f32)).T
        for h in range(heads):
            dlt[h:h+1,rows]=jnp.sum(prod[h*HD:(h+1)*HD],axis=0,keepdims=True)
    dks[...]=jnp.zeros_like(dks); dvs[...]=jnp.zeros_like(dvs)
    kio=lax.broadcasted_iota(jnp.int32,(QB,QB),0)
    qio=lax.broadcasted_iota(jnp.int32,(QB,QB),1)
    def qblock(i,_):
        at=pl.multiple_of(i*QB,QB)
        qr=pl.ds(at,QB)
        srow=st_ref[:,qr]
        dqs[...]=jnp.zeros_like(dqs)
        def step(mode,j,carry):
            kat=pl.multiple_of(j*QB,QB); kr=pl.ds(kat,QB)
            if mode:
                mask=kio>=(srow-kat)
                if mode==2: mask=mask&(kio<=qio)
            for g in range(pairs):
                lanes=slice(g*128,(g+1)*128)
                ps=[];dss=[]
                for e in range(2):
                    h=2*g+e; sub=slice(h*HD,(h+1)*HD)
                    s=lax.dot_general(ks[kr,lanes],qm[e,qr,lanes],NT,preferred_element_type=f32)
                    if mode: s=jnp.where(mask,s,NEG)
                    p=jnp.exp(s-lse_ref[h:h+1,qr])
                    dp=lax.dot_general(vs[kr,lanes],dom[e,qr,lanes],NT,preferred_element_type=f32)
                    d=(p*(dp-dlt[h:h+1,qr])).astype(bf)
                    dqs[sub]+=jnp.dot(kt[sub,kr],d,preferred_element_type=f32)
                    ps.append(p.astype(bf)); dss.append(d)
                dcat=jnp.concatenate([dom[0,qr,lanes],dom[1,qr,lanes]],axis=0)
                qcat=jnp.concatenate([qm[0,qr,lanes],qm[1,qr,lanes]],axis=0)
                dvs[kr,lanes]+=jnp.dot(jnp.concatenate(ps,axis=1),dcat,preferred_element_type=f32)
                dks[kr,lanes]+=jnp.dot(jnp.concatenate(dss,axis=1),qcat,preferred_element_type=f32)
            return carry
        step(2,i,0)
        lax.fori_loop(info[1+i],info[1+nb+i],functools.partial(step,1),0)
        lax.fori_loop(info[1+nb+i],i,functools.partial(step,0),0)
        qm[0,qr]=(dqs[...]*(HD**-0.5)).T.astype(bf)
        return 0
    lax.fori_loop(0,nb,qblock,0)
    for dst,base in ((dkeep,c*half),(dsend,(1-c)*half)):
        rows=pl.ds(pl.multiple_of(base,half),half)
        dst[:,:cols]=qm[0,rows]
        dst[:,cols:2*cols]=dks[rows].astype(bf)
        dst[:,2*cols:]=dvs[rows].astype(bf)

def attn_bwd(own,recv,do_own,do_recv,o_own,o_recv,starts,lse,info):
    half,cols=own.shape[0],own.shape[1]//3; n=2*half
    return pl.pallas_call(bwd_kernel,
        in_specs=[SM]+[VM]*8, out_specs=[VM]*2,
        scratch_shapes=[pltpu.VMEM((2,n,cols),bf),pltpu.VMEM((n,cols),bf),pltpu.VMEM((n,cols),bf),pltpu.VMEM((cols,n),bf),pltpu.VMEM((2,n,cols),bf),pltpu.VMEM((cols//HD,n),f32),
                            pltpu.VMEM((cols,QB),f32),pltpu.VMEM((n,cols),f32),pltpu.VMEM((n,cols),f32)],
        out_shape=[jax.ShapeDtypeStruct((half,3*cols),bf)]*2,
        cost_estimate=pl.CostEstimate(flops=2*5*n*n//3*cols,bytes_accessed=16*half*cols*2,transcendentals=n*n*6//3),
        compiler_params=pltpu.CompilerParams(vmem_limit_bytes=56<<20),
    )(info,own,recv,do_own,do_recv,o_own,o_recv,starts,lse)


def dot(left, right, dims=(((1,), (0,)), ((), ()))):
    return lax.dot_general(left, right, dims, preferred_element_type=f32)


def phase_order(dp_size, last):
    high = [1 << k for k in range(dp_size.bit_length() - 2, 1, -1)]
    return high + ([2, 0, 1] if last == "tensor" else [0, 2, 1]) if dp_size > 2 else [0, 1]


def exchange(value, bit, dp_size):
    if bit:
        return lax.ppermute(value, "dp", [(i, i ^ bit) for i in range(dp_size)])
    return lax.ppermute(value, "tensor", [(0, 1), (1, 0)])


def gather_blocks(shard, order, dp_size):
    held = shard[None]
    for bit in order:
        held = jnp.concatenate([held, exchange(held, bit, dp_size)], axis=0)
    return held


def scatter_sum(partial, order, dp_size):
    kept = partial
    for bit in reversed(order):
        n = kept.shape[0] // 2
        got = exchange(kept[n:], bit, dp_size)
        kept = (kept[:n].astype(f32) + got.astype(f32)).astype(bf)
    return kept[0]


def positions(order, dp_size, dp_pos, tensor_pos):
    d = jnp.arange(dp_size, dtype=jnp.int32) ^ dp_pos
    out = []
    for t in range(2):
        place = jnp.zeros((dp_size,), jnp.int32)
        for k, bit in enumerate(order):
            on = ((d & bit) != 0).astype(jnp.int32) if bit else (tensor_pos != t).astype(jnp.int32)
            place = place + (on << k)
        out.append(place)
    return jnp.concatenate(out)


def move_kernel(table, source, out):
    out[...] = source[...]


def move_blocks(blocks, table, scatter):
    count, rows, cols = blocks.shape
    one, other = (lambda g, s: (g, 0, 0)), (lambda g, s: (s[g], 0, 0))
    return pl.pallas_call(
        move_kernel,
        grid_spec=pltpu.PrefetchScalarGridSpec(
            num_scalar_prefetch=1,
            grid=(count,),
            in_specs=[pl.BlockSpec((1, rows, cols), one if scatter else other)],
            out_specs=pl.BlockSpec((1, rows, cols), other if scatter else one),
        ),
        out_shape=jax.ShapeDtypeStruct(blocks.shape, blocks.dtype),
        cost_estimate=pl.CostEstimate(flops=0, bytes_accessed=4 * blocks.size, transcendentals=0),
    )(table, blocks)


def layer_norm_parts(values):
    centered = values - jnp.mean(values, axis=-1, keepdims=True)
    inverse = lax.rsqrt(jnp.mean(centered * centered, axis=-1, keepdims=True) + EPSILON)
    return centered * inverse, inverse


def layer_norm_back(hat, inverse, gain, grad):
    scaled = grad * gain
    back = inverse * (
        scaled
        - jnp.mean(scaled, axis=-1, keepdims=True)
        - hat * jnp.mean(scaled * hat, axis=-1, keepdims=True)
    )
    return back, jnp.sum(grad * hat, axis=0), jnp.sum(grad, axis=0)


def gelu_parts(pre):
    root = 0.7978845608
    inner = jnp.tanh(root * (pre + 0.044715 * pre * pre * pre))
    value = 0.5 * pre * (1.0 + inner)
    slope = 0.5 * (1.0 + inner) + 0.5 * pre * (1.0 - inner * inner) * root * (
        1.0 + 3 * 0.044715 * pre * pre
    )
    return value, slope


def on_device(
    tokens, segment_ids, ln1_gain, ln1_bias, w_qkv, b_qv, w_attn_out, b_attn_out,
    ln2_gain, ln2_bias, w_fc, b_fc, w_proj, b_proj, cotangent,
):
    dp_size = lax.axis_size("dp")
    dp_pos, t_pos = lax.axis_index("dp"), lax.axis_index("tensor")
    core = dp_pos % 2
    rows = ln1_gain.shape[0]
    width = tokens.shape[1]
    cols = w_qkv.shape[2]
    hidden = w_fc.shape[1]
    fan = b_fc.shape[0] // rows
    first, second = phase_order(dp_size, "tensor"), phase_order(dp_size, "x")
    swap = []
    for d in range(dp_size):
        for t in range(2):
            swap.append((2 * d + t, 2 * (d - d % 2 + t) + d % 2))
    mine = core == t_pos

    residual_in = lax.ppermute(tokens, BOTH, swap)
    seg_other = lax.ppermute(segment_ids, "dp", [(i, i ^ 1) for i in range(dp_size)])
    seg = jnp.where(mine, segment_ids, seg_other)[0]
    small = jnp.concatenate(
        [ln1_gain[:, None], ln1_bias[:, None], b_qv.T, b_attn_out[:, None], ln2_gain[:, None],
         ln2_bias[:, None], b_proj[:, None], b_fc.reshape(rows, fan)], axis=1)
    small = jnp.pad(small, ((0, 0), (0, SMALL - small.shape[1])))
    pack_a = jnp.concatenate([w_qkv.reshape(rows, 3 * cols), w_attn_out.T, small], axis=1)
    place_a = positions(first, dp_size, dp_pos, t_pos)
    place_b = positions(second, dp_size, dp_pos, t_pos)
    all_a = move_blocks(gather_blocks(pack_a, first, dp_size), place_a, False).reshape(2, width, -1)
    all_fc = move_blocks(gather_blocks(w_fc, first, dp_size), place_a, False).reshape(2, width, hidden)
    all_proj = move_blocks(gather_blocks(w_proj.T, second, dp_size), place_b, False).reshape(2, width, hidden)
    qkv_w = all_a[:, :, : 3 * cols]
    out_w = all_a[:, :, 3 * cols : 4 * cols]
    vec = all_a[0, :, 4 * cols :].astype(f32).T
    gain1, bias1, b_q, b_v, out_bias, gain2, bias2, proj_bias = (vec[k] for k in range(8))
    fc_bias = vec[8 : 8 + fan].T.reshape(2, hidden)
    qkv_bias = jnp.stack([b_q.reshape(2, cols), jnp.zeros((2, cols), f32), b_v.reshape(2, cols)], axis=1).reshape(2, 3 * cols)

    x = residual_in.astype(f32)
    hat1, inv1 = layer_norm_parts(x)
    n1 = (hat1 * gain1 + bias1).astype(bf)
    take = lambda arr, k: lax.dynamic_index_in_dim(arr, k, 0, keepdims=False)
    other = 1 - core
    qkv_send = (dot(n1, take(qkv_w, other)) + take(qkv_bias, other)).astype(bf)
    qkv_recv = exchange(qkv_send, 1, dp_size)
    qkv_own = (dot(n1, take(qkv_w, core)) + take(qkv_bias, core)).astype(bf)
    starts, info = attn_info(seg, core)
    o_own, o_send, lse = attn_fwd(qkv_own, qkv_recv, starts, info)
    o_recv = exchange(o_send, 1, dp_size)
    wo_own, wo_other = take(out_w, core), take(out_w, other)
    branch = dot(o_own, wo_own, NT) + dot(o_recv, wo_other, NT) + out_bias
    middle = x + BRANCH_SCALE * branch
    hat2, inv2 = layer_norm_parts(middle)
    n2 = (hat2 * gain2 + bias2).astype(bf)
    grad_out = lax.ppermute(cotangent, BOTH, swap).astype(f32)
    scaled_out = BRANCH_SCALE * grad_out
    d_b_proj = jnp.sum(scaled_out, axis=0)
    d_mlp = scaled_out.astype(bf)
    mlp = jnp.zeros_like(x)
    d_n2 = jnp.zeros_like(x)
    d_fc, d_proj, d_b_fc = [], [], []
    for t in range(2):
        act, slope = gelu_parts(dot(n2, all_fc[t]) + fc_bias[t])
        act = act.astype(bf)
        mlp = mlp + dot(act, all_proj[t], NT)
        d_pre = dot(d_mlp, all_proj[t]) * slope
        d_b_fc.append(jnp.sum(d_pre, axis=0))
        d_pre = d_pre.astype(bf)
        d_n2 = d_n2 + dot(d_pre, all_fc[t], NT)
        d_fc.append(dot(n2, d_pre, TN).astype(bf))
        d_proj.append(dot(d_mlp, act, TN).astype(bf))
    block_out = (middle + BRANCH_SCALE * (mlp + proj_bias)).astype(bf)
    block_out = lax.ppermute(block_out, BOTH, swap)
    blocks = lambda parts: jnp.stack(parts).reshape(2 * dp_size, rows, -1)
    sum_fc = scatter_sum(move_blocks(blocks(d_fc), place_a, True), first, dp_size)
    sum_proj = scatter_sum(move_blocks(blocks(d_proj), place_b, True), second, dp_size)

    back2, d_gain2, d_bias2 = layer_norm_back(hat2, inv2, gain2, d_n2)
    d_middle = grad_out + back2
    scaled_mid = BRANCH_SCALE * d_middle
    d_b_out = jnp.sum(scaled_mid, axis=0)
    d_attn = scaled_mid.astype(bf)
    do_send = dot(d_attn, wo_other).astype(bf)
    do_recv = exchange(do_send, 1, dp_size)
    do_own = dot(d_attn, wo_own).astype(bf)
    dwo_own = dot(d_attn, o_own, TN).astype(bf)
    dwo_other = dot(d_attn, o_recv, TN).astype(bf)
    dq_own, dq_send = attn_bwd(qkv_own, qkv_recv, do_own, do_recv, o_own, o_send, starts, lse, info)
    dq_recv = exchange(dq_send, 1, dp_size)
    d_n1 = dot(dq_own, take(qkv_w, core), NT) + dot(dq_recv, take(qkv_w, other), NT)
    dwq_own = dot(n1, dq_own, TN).astype(bf)
    dwq_other = dot(n1, dq_recv, TN).astype(bf)
    back1, d_gain1, d_bias1 = layer_norm_back(hat1, inv1, gain1, d_n1)
    grad_tokens = lax.ppermute((d_middle + back1).astype(bf), BOTH, swap)
    s_own = jnp.sum(dq_own.astype(f32), axis=0).reshape(3, cols)
    s_other = jnp.sum(dq_recv.astype(f32), axis=0).reshape(3, cols)
    pick = lambda a, b: jnp.where(core == 0, jnp.concatenate([a, b]), jnp.concatenate([b, a]))
    d_small = jnp.stack(
        [d_gain1, d_bias1, pick(s_own[0], s_other[0]), pick(s_own[2], s_other[2]), d_b_out, d_gain2, d_bias2, d_b_proj], axis=1)
    d_small = jnp.concatenate(
        [d_small, jnp.concatenate(d_b_fc).reshape(width, fan), jnp.zeros((width, SMALL - 8 - fan), f32)], axis=1).astype(bf)
    own_a = jnp.concatenate([dwq_own, dwo_own, d_small], axis=1)
    other_a = jnp.concatenate([dwq_other, dwo_other, d_small], axis=1)
    part_a = jnp.where(core == 0, jnp.stack([own_a, other_a]), jnp.stack([other_a, own_a])).reshape(2 * dp_size, rows, -1)
    sum_a = scatter_sum(move_blocks(part_a, place_a, True), first, dp_size).astype(f32)
    vecs = sum_a[:, 4 * cols :]
    return (
        block_out,
        grad_tokens,
        vecs[:, 0],
        vecs[:, 1],
        sum_a[:, : 3 * cols].reshape(rows, 3, cols),
        vecs[:, 2:4].T,
        sum_a[:, 3 * cols : 4 * cols].T,
        vecs[:, 4],
        vecs[:, 5],
        vecs[:, 6],
        sum_fc.astype(f32),
        vecs[:, 8 : 8 + fan].reshape(rows * fan),
        sum_proj.astype(f32).T,
        vecs[:, 7],
    )


def solution(mesh):
    vec, tok = P("dp"), P(BOTH, None)
    in_specs = (
        tok, P("dp", None), vec, vec, P("dp", None, "tensor"), P(None, "dp"), P("tensor", "dp"),
        vec, vec, vec, P("dp", "tensor"), vec, P("tensor", "dp"), vec, tok,
    )
    out_specs = (
        tok, tok, vec, vec, P("dp", None, "tensor"), P(None, "dp"), P("tensor", "dp"),
        vec, vec, vec, P("dp", "tensor"), vec, P("tensor", "dp"), vec,
    )
    return jax.shard_map(on_device, mesh=mesh, in_specs=in_specs, out_specs=out_specs, check_vma=False)
```

time: 1500 us -> 667 us (0.44)
  waiting for transfers between devices: 608 us -> 141 us
  matrix products: 437 us -> 94.8 us
  Pallas kernels: 0 us -> 208 us
  blocking collectives: 169 us -> 0 us
  other arithmetic: 126 us -> 48.5 us
  starting transfers between devices: 0.87 us -> 62.8 us
  loops' own time: 29.1 us -> 0 us
  between operations: 17.5 us -> 2.02 us
    reduce_scatter x8 -> x0, waiting for transfers between devices: 390 us -> none  [the longest x1 78.9 us: on_device(): lax.psum_scatter(d_fc_w, 'dp', scatter_dimension=0, tiled=True)]
    dot_general x182 -> x24, matrix products: 437 us -> 94.8 us  [dot(): return lax.dot_general(left, right, dims, preferred_element_type=f32)]
    all_gather x7 -> x0, waiting for transfers between devices: 216 us -> none  [the longest x1 45.9 us: on_device(): full_two = lax.all_gather(normed_two, 'tensor', axis=0, tiled=True)]
    pallas_call x0 -> x8, Pallas kernels: none -> 208 us  [the longest x6 113 us: move_blocks(): pl.pallas_call(move_kernel, grid_spec=pltpu.PrefetchScalarGridSpec(num_sc...]
    ppermute x0 -> x39, waiting for transfers between devices: none -> 141 us  [the longest x6 104 us: exchange(): return lax.ppermute(value, 'tensor', [(0, 1), (1, 0)])]
    unnamed x2 -> x0, blocking collectives: 123 us -> none
    ppermute x0 -> x39, starting transfers between devices: none -> 62.8 us  [the longest x28 25.9 us: exchange(): return lax.ppermute(value, 'dp', [(i, i ^ bit) for i in range(dp_size)])]
    add x36 -> x2, other arithmetic: 45 us -> 0.02 us  [positions(): place = place + (on << k)]
  transfers between devices with their start and end apart: 16 -> 39, of which waited for: 13 -> 14; matrix products, arithmetic and copies ran while one was open for 6% -> 28% of each run, Pallas kernels for 0% -> 32%
where the time goes in v1:
time: 667 us; the launch traced here: 657 us
  Pallas kernels  208 us (31%)
  waiting for transfers between devices  141 us (21%)
  local copies, waits for them, and re-layouts  100 us (15%)
  matrix products  94.8 us (14%)
  starting transfers between devices  62.8 us (9%)
  other arithmetic  48.5 us (7%)
    pallas_call x6, Pallas kernels, move_blocks(): pl.pallas_call(move_kernel, grid_spec=pltpu.PrefetchScalarGridSpec(num_sc...  113 us
    ppermute x6, waiting for transfers between devices, exchange(): return lax.ppermute(value, 'tensor', [(0, 1), (1, 0)])  104 us
    dot_general x24, matrix products, dot(): return lax.dot_general(left, right, dims, preferred_element_type=f32)  94.8 us
    pallas_call x1, Pallas kernels, attn_bwd(): pl.pallas_call(bwd_kernel, in_specs=[SM] + [VM] * 8, out_specs=[VM] * 2,...  50.2 us
    pallas_call x1, Pallas kernels, attn_fwd(): pl.pallas_call(fwd_kernel, in_specs=[SM, VM, VM, VM], out_specs=[VM] * 3,...  44.5 us
    ppermute x28, waiting for transfers between devices, exchange(): return lax.ppermute(value, 'dp', [(i, i ^ bit) for i in range(dp_size)])  37.5 us
    ppermute x28, starting transfers between devices, exchange(): return lax.ppermute(value, 'dp', [(i, i ^ bit) for i in range(dp_size)])  25.9 us
    unnamed x131, local copies, waits for them, and re-layouts  23.5 us
  transfers between devices with their start and end apart: 39, of which 14 were waited for; matrix products, arithmetic and copies ran while one was open for 28% of the time, Pallas kernels for 32%

profile of v1, /device:TPU:0, one launch (start us, length us, event | category | flops | bytes accessed | tf_op | source)
XLA Modules:
  0.0 657.3 jit_solution(6238898686212099971)
XLA Ops:
  26.4 13.3 %collective-permute-start.20 = (bf16[1024,768]{0,1:T(8,128)(2,1)}, bf16[1024,768]{0,1:T(8,128)(2,1)}, u32[]{:S(2)}, u32[]{:S(2)}) collective-permute-start(bf16[1024,768]{0,1:T(8,128)(2,1)} %copy.195), channel_id=1, source_target_pairs={{0,0},{1,2},{2,1},{3,3},{4,4},{5,6},{6,5},{7,7},{8,8},{9,10},{10,9... | collective-permute-start | bytes 4718600 | tf_op jit(solution)/shard_map/ppermute | solution.py:312
  42.0 6.3 collective-permute-done.3
  51.6 7.4 %collective-permute-done.4 = bf16[4,48,1664]{2,1,0:T(8,128)(2,1)S(1)} collective-permute-done((bf16[4,48,1664]{2,1,0:T(8,128)(2,1)S(1)}, bf16[4,48,1664]{2,1,0:T(8,128)(2,1)S(1)}, u32[]{:S(2)}, u32[]{:S(2)}) %collective-permute-start.4) | collective-permute-done | bytes 639008 | tf_op jit(solution)/shard_map/ppermute | solution.py:179
  65.4 24.7 %collective-permute-done.5 = bf16[8,48,1664]{2,1,0:T(8,128)(2,1)S(1)} collective-permute-done((bf16[8,48,1664]{2,1,0:T(8,128)(2,1)S(1)}, bf16[8,48,1664]{2,1,0:T(8,128)(2,1)S(1)}, u32[]{:S(2)}, u32[]{:S(2)}) %collective-permute-start.5) | collective-permute-done | bytes 1277984 | tf_op jit(solution)/shard_map/ppermute | solution.py:180
  92.7 10.1 %collective-permute-done.16 = bf16[4,48,1536]{2,1,0:T(8,128)(2,1)S(1)} collective-permute-done((bf16[4,48,1536]{2,1,0:T(8,128)(2,1)S(1)}, bf16[4,48,1536]{2,1,0:T(8,128)(2,1)S(1)}, u32[]{:S(2)}, u32[]{:S(2)}) %collective-permute-start.16) | collective-permute-done | bytes 589856 | tf_op jit(solution)/shard_map/ppermute | solution.py:180
  106.8 19.6 %collective-permute-done.12 = bf16[8,48,1536]{2,1,0:T(8,128)(2,1)S(1)} collective-permute-done((bf16[8,48,1536]{2,1,0:T(8,128)(2,1)S(1)}, bf16[8,48,1536]{2,1,0:T(8,128)(2,1)S(1)}, u32[]{:S(2)}, u32[]{:S(2)}) %collective-permute-start.12) | collective-permute-done | bytes 1179680 | tf_op jit(solution)/shard_map/ppermute | solution.py:180
  131.9 19.0 %shard_map.254 = bf16[32,48,1664]{2,1,0:T(8,128)(2,1)} custom-call(s32[32]{0:T(128)} %pad_add_fusion.1.table, bf16[32,48,1664]{2,1,0:T(8,128)(2,1)} %constant_dynamic-update-slice_fusion.5.source), custom_call_target="tpu_custom_call" | custom-call | bytes 10223616 | tf_op jit(solution)/shard_map/pallas_call | solution.py:218
  156.9 5.3 add_convert_fusion.3
  166.3 18.7 %shard_map.256 = bf16[32,48,1536]{2,1,0:T(8,128)(2,1)} custom-call(s32[32]{0:T(128)} %pad_add_fusion.1.table, bf16[32,48,1536]{2,1,0:T(8,128)(2,1)} %constant_dynamic-update-slice_fusion.16.source), custom_call_target="tpu_custom_call" | custom-call | bytes 9437184 | tf_op jit(solution)/shard_map/pallas_call | solution.py:218
  188.3 18.7 %shard_map.257 = bf16[32,48,1536]{2,1,0:T(8,128)(2,1)} custom-call(s32[32]{0:T(128)} %pad_add_fusion.2.table, bf16[32,48,1536]{2,1,0:T(8,128)(2,1)} %constant_dynamic-update-slice_fusion.27.source), custom_call_target="tpu_custom_call" | custom-call | bytes 9437184 | tf_op jit(solution)/shard_map/pallas_call | solution.py:218
  207.0 5.1 fusion.93
  214.7 44.5 %shard_map.255 = (bf16[1024,384]{1,0:T(8,128)(2,1)S(1)}, bf16[1024,384]{1,0:T(8,128)(2,1)S(1)}, f32[6,2048]{1,0:T(8,128)S(1)}) custom-call(s32[17]{0:T(128)S(1)} %pad_add_fusion.info, bf16[1024,1152]{1,0:T(8,128)(2,1)S(1)} %add_convert_fusion.4.own, bf16[1024,1152]{1,0:T(8,128)(2,1)} %collective-permute-done.7.recv, s32[1,2048]{1,0:T(1,128)S(1)} %bitcast.135), custom_call_target="tpu_custom_call" | custom-call | flops 2147483520 | bytes 6291456 | tf_op jit(solution)/shard_map/pallas_call | solution.py:87
  277.8 9.1 %fusion.100 = (bf16[1536]{0:T(1024)(128)(2,1)S(1)}, bf16[1024,1536]{1,0:T(8,128)(2,1)S(1)}) fusion(f32[1024,1536]{1,0:T(8,128)S(1)} %get-tuple-element.172, f32[1536]{0:T(1024)S(1)} %add.315, bf16[768,1536]{1,0:T(8,128)(2,1)S(1)} %bitcast.159, bf16[1024,768]{0,1:T(8,128)(2,1)} %collective-permute-done.20), kind=kOutput, calls=%fused_computation.255 | convolution fusion | flops 2451307008 | bytes 13378560 | tf_op jit(solution)/shard_map/dot_general | solution.py:169
  289.7 8.7 %fusion.99 = (bf16[1536]{0:T(1024)(128)(2,1)}, bf16[1024,1536]{1,0:T(8,128)(2,1)S(1)}) fusion(f32[1024,1536]{1,0:T(8,128)S(1)} %fusion.101, f32[1536]{0:T(1024)S(1)} %add.302, bf16[768,1536]{1,0:T(8,128)(2,1)S(1)} %bitcast.157, bf16[1024,768]{0,1:T(8,128)(2,1)} %collective-permute-done.20), kind=kOutput, calls=%fused_computation.254 | convolution fusion | flops 2451307008 | bytes 13378560 | tf_op jit(solution)/shard_map/dot_general | solution.py:169
  324.1 13.3 %collective-permute-start.19 = (bf16[1024,768]{0,1:T(8,128)(2,1)}, bf16[1024,768]{0,1:T(8,128)(2,1)}, u32[]{:S(2)}, u32[]{:S(2)}) collective-permute-start(bf16[1024,768]{0,1:T(8,128)(2,1)} %add_convert_fusion.5), channel_id=1, source_target_pairs={{0,0},{1,2},{2,1},{3,3},{4,4},{5,6},{6,5},{7,7},{8,8},{9,10},{10,9... | collective-permute-start | bytes 4718600 | tf_op jit(solution)/shard_map/ppermute | solution.py:330
  346.0 19.1 %shard_map.260 = bf16[32,48,1536]{2,1,0:T(8,128)(2,1)} custom-call(s32[32]{0:T(128)} %pad_add_fusion.1.table, bf16[32,48,1536]{2,1,0:T(8,128)(2,1)} %bitcast.146), custom_call_target="tpu_custom_call" | custom-call | bytes 9437184 | tf_op jit(solution)/shard_map/pallas_call | solution.py:218
  368.8 6.2 fusion.31
  375.1 50.2 %shard_map.258 = (bf16[1024,1152]{1,0:T(8,128)(2,1)}, bf16[1024,1152]{1,0:T(8,128)(2,1)}) custom-call(s32[17]{0:T(128)} %copy-done.3, bf16[1024,1152]{1,0:T(8,128)(2,1)} %copy-done.5, bf16[1024,1152]{1,0:T(8,128)(2,1)} %collective-permute-done.7.recv, bf16[1024,384]{1,0:T(8,128)(2,1)} %convolution_convert_fusion.7.doo, ...), custom_call_target="tpu_custom_call" | custom-call | flops 5368709120 | bytes 12582912 | tf_op jit(solution)/shard_map/pallas_call | solution.py:158
  425.3 5.0 fusion.32
  432.9 18.7 %shard_map.261 = bf16[32,48,1536]{2,1,0:T(8,128)(2,1)} custom-call(s32[32]{0:T(128)} %pad_add_fusion.2.table, bf16[32,48,1536]{2,1,0:T(8,128)(2,1)} %bitcast.145), custom_call_target="tpu_custom_call" | custom-call | bytes 9437184 | tf_op jit(solution)/shard_map/pallas_call | solution.py:218
  469.1 5.0 fusion.27
  489.1 5.8 convolution_convert_fusion.4
  495.6 6.0 concatenate.171
  501.6 6.0 concatenate.170
  507.5 7.9 %maximum_select_fusion = bf16[2,768,1664]{2,1,0:T(8,128)(2,1)} fusion(bf16[1,768,1664]{2,1,0:T(8,128)(2,1)} %bitcast.147, bf16[1,768,1664]{2,1,0:T(8,128)(2,1)} %bitcast.148, pred[]{:T(512)S(6)} %eq.33), kind=kLoop, calls=%fused_computation.18 | loop fusion | flops 7667712 | bytes 10223617 | tf_op jit(solution)/shard_map/jit(_where)/select_n | solution.py:361
  515.5 19.0 %shard_map.259 = bf16[32,48,1664]{2,1,0:T(8,128)(2,1)} custom-call(s32[32]{0:T(128)} %pad_add_fusion.1.table, bf16[32,48,1664]{2,1,0:T(8,128)(2,1)} %bitcast.137), custom_call_target="tpu_custom_call" | custom-call | bytes 10223616 | tf_op jit(solution)/shard_map/pallas_call | solution.py:218
  554.2 17.7 %collective-permute-done.30 = bf16[8,48,1536]{2,1,0:T(8,128)(2,1)} collective-permute-done((bf16[8,48,1536]{2,1,0:T(8,128)(2,1)}, bf16[8,48,1536]{2,1,0:T(8,128)(2,1)}, u32[]{:S(2)}, u32[]{:S(2)}) %collective-permute-start.30) | collective-permute-done | bytes 1179680 | tf_op jit(solution)/shard_map/ppermute | solution.py:180
  591.4 5.1 collective-permute-done.36
  597.0 26.5 %collective-permute-done.25 = bf16[8,48,1664]{2,1,0:T(8,128)(2,1)S(1)} collective-permute-done((bf16[8,48,1664]{2,1,0:T(8,128)(2,1)S(1)}, bf16[8,48,1664]{2,1,0:T(8,128)(2,1)S(1)}, u32[]{:S(2)}, u32[]{:S(2)}) %collective-permute-start.25) | collective-permute-done | bytes 1277984 | tf_op jit(solution)/shard_map/ppermute | solution.py:180
  629.2 8.8 %collective-permute-done.26 = bf16[4,48,1664]{2,1,0:T(8,128)(2,1)S(1)} collective-permute-done((bf16[4,48,1664]{2,1,0:T(8,128)(2,1)S(1)}, bf16[4,48,1664]{2,1,0:T(8,128)(2,1)S(1)}, u32[]{:S(2)}, u32[]{:S(2)}) %collective-permute-start.26) | collective-permute-done | bytes 639008 | tf_op jit(solution)/shard_map/ppermute | solution.py:179
  639.1 6.3 collective-permute-done.27
  647.8 5.5 collective-permute-done.28
  (349 shorter events, 212.7 us)
Async XLA Ops:
  8.6 31.0 %collective-permute-start.2 = (bf16[1,48,1664]{2,1,0:T(8,128)(2,1)S(1)}, bf16[1,48,1664]{2,1,0:T(8,128)(2,1)S(1)}, u32[]{:S(2)}, u32[]{:S(2)}) collective-permute-start(bf16[1,48,1664]{2,1,0:T(8,128)(2,1)S(1)} %fusion.66), channel_id=1, source_target_pairs={{0,16},{2,18},{4,20},{6,22},{8,24},{10,26},{12,28},{14,30},{16,0},... | collective-permute-start | bytes 479240 | tf_op jit(solution)/shard_map/ppermute | solution.py:179
  12.7 13.6 %collective-permute-start.1 = (s32[1,2048]{1,0:T(1,128)}, s32[1,2048]{1,0:T(1,128)S(1)}, u32[]{:S(2)}, u32[]{:S(2)}) collective-permute-start(s32[1,2048]{1,0:T(1,128)} %param.16), channel_id=1, source_target_pairs={{0,2},{2,0},{4,6},{6,4},{8,10},{10,8},{12,14},{14,12},{16,18},{18,... | collective-permute-start | bytes 24584 | tf_op jit(solution)/shard_map/ppermute | solution.py:277
  15.3 90.7 %collective-permute-start = (bf16[1024,768]{0,1:T(8,128)(2,1)}, bf16[1024,768]{0,1:T(8,128)(2,1)S(1)}, u32[]{:S(2)}, u32[]{:S(2)}) collective-permute-start(bf16[1024,768]{0,1:T(8,128)(2,1)} %copy.181), channel_id=1, source_target_pairs={{0,0},{1,2},{2,1},{3,3},{4,4},{5,6},{6,5},{7,7},{8,8},{9,10},{10,9... | collective-permute-start | bytes 4718600 | tf_op jit(solution)/shard_map/ppermute | solution.py:276
  17.4 24.1 %collective-permute-start.9 = (bf16[1,48,1536]{2,1,0:T(8,128)(2,1)S(1)}, bf16[1,48,1536]{2,1,0:T(8,128)(2,1)S(1)}, u32[]{:S(2)}, u32[]{:S(2)}) collective-permute-start(bf16[1,48,1536]{2,1,0:T(8,128)(2,1)S(1)} %bitcast.149), channel_id=1, source_target_pairs={{0,16},{2,18},{4,20},{6,22},{8,24},{10,26},{12,28},{14,30},{16,0},... | collective-permute-start | bytes 442376 | tf_op jit(solution)/shard_map/ppermute | solution.py:179
  17.5 31.8 %collective-permute-start.14 = (bf16[1,48,1536]{2,1,0:T(8,128)(2,1)S(1)}, bf16[1,48,1536]{2,1,0:T(8,128)(2,1)S(1)}, u32[]{:S(2)}, u32[]{:S(2)}) collective-permute-start(bf16[1,48,1536]{2,1,0:T(8,128)(2,1)S(1)} %bitcast.153), channel_id=1, source_target_pairs={{0,16},{2,18},{4,20},{6,22},{8,24},{10,26},{12,28},{14,30},{16,0},... | collective-permute-start | bytes 442376 | tf_op jit(solution)/shard_map/ppermute | solution.py:179
  26.4 251.4 %collective-permute-start.20 = (bf16[1024,768]{0,1:T(8,128)(2,1)}, bf16[1024,768]{0,1:T(8,128)(2,1)}, u32[]{:S(2)}, u32[]{:S(2)}) collective-permute-start(bf16[1024,768]{0,1:T(8,128)(2,1)} %copy.195), channel_id=1, source_target_pairs={{0,0},{1,2},{2,1},{3,3},{4,4},{5,6},{6,5},{7,7},{8,8},{9,10},{10,9... | collective-permute-start | bytes 4718600 | tf_op jit(solution)/shard_map/ppermute | solution.py:312
  41.5 18.3 %collective-permute-start.10 = (bf16[2,48,1536]{2,1,0:T(8,128)(2,1)S(1)}, bf16[2,48,1536]{2,1,0:T(8,128)(2,1)S(1)}, u32[]{:S(2)}, u32[]{:S(2)}) collective-permute-start(bf16[2,48,1536]{2,1,0:T(8,128)(2,1)S(1)} %pad_maximum_fusion.9), channel_id=1, source_target_pairs={{0,8},{2,10},{4,12},{6,14},{8,0},{10,2},{12,4},{14,6},{16,24},{18,... | collective-permute-start | bytes 884744 | tf_op jit(solution)/shard_map/ppermute | solution.py:179
  59.1 31.1 %collective-permute-start.5 = (bf16[8,48,1664]{2,1,0:T(8,128)(2,1)S(1)}, bf16[8,48,1664]{2,1,0:T(8,128)(2,1)S(1)}, u32[]{:S(2)}, u32[]{:S(2)}) collective-permute-start(bf16[8,48,1664]{2,1,0:T(8,128)(2,1)S(1)} %pad_maximum_fusion.2), channel_id=1, source_target_pairs={{0,1},{1,0},{2,3},{3,2},{4,5},{5,4},{6,7},{7,6},{8,9},{9,8},{10,11... | collective-permute-start | bytes 3833864 | tf_op jit(solution)/shard_map/ppermute | solution.py:180
  59.9 32.4 %collective-permute-start.11 = (bf16[4,48,1536]{2,1,0:T(8,128)(2,1)S(1)}, bf16[4,48,1536]{2,1,0:T(8,128)(2,1)S(1)}, u32[]{:S(2)}, u32[]{:S(2)}) collective-permute-start(bf16[4,48,1536]{2,1,0:T(8,128)(2,1)S(1)} %pad_maximum_fusion.6), channel_id=1, source_target_pairs={{0,4},{2,6},{4,0},{6,2},{8,12},{10,14},{12,8},{14,10},{16,20},{18,... | collective-permute-start | bytes 1769480 | tf_op jit(solution)/shard_map/ppermute | solution.py:179
  60.8 42.0 %collective-permute-start.16 = (bf16[4,48,1536]{2,1,0:T(8,128)(2,1)S(1)}, bf16[4,48,1536]{2,1,0:T(8,128)(2,1)S(1)}, u32[]{:S(2)}, u32[]{:S(2)}) collective-permute-start(bf16[4,48,1536]{2,1,0:T(8,128)(2,1)S(1)} %pad_maximum_fusion.7), channel_id=1, source_target_pairs={{0,1},{1,0},{2,3},{3,2},{4,5},{5,4},{6,7},{7,6},{8,9},{9,8},{10,11... | collective-permute-start | bytes 1769480 | tf_op jit(solution)/shard_map/ppermute | solution.py:180
  91.4 38.8 %collective-permute-start.6 = (bf16[16,48,1664]{2,1,0:T(8,128)(2,1)S(1)}, bf16[16,48,1664]{2,1,0:T(8,128)(2,1)S(1)}, u32[]{:S(2)}, u32[]{:S(2)}) collective-permute-start(bf16[16,48,1664]{2,1,0:T(8,128)(2,1)S(1)} %get-tuple-element.129), channel_id=1, source_target_pairs={{0,2},{2,0},{4,6},{6,4},{8,10},{10,8},{12,14},{14,12},{16,18},{18,... | collective-permute-start | bytes 7667720 | tf_op jit(solution)/shard_map/ppermute | solution.py:179
  92.5 33.9 %collective-permute-start.12 = (bf16[8,48,1536]{2,1,0:T(8,128)(2,1)S(1)}, bf16[8,48,1536]{2,1,0:T(8,128)(2,1)S(1)}, u32[]{:S(2)}, u32[]{:S(2)}) collective-permute-start(bf16[8,48,1536]{2,1,0:T(8,128)(2,1)S(1)} %pad_maximum_fusion.3), channel_id=1, source_target_pairs={{0,1},{1,0},{2,3},{3,2},{4,5},{5,4},{6,7},{7,6},{8,9},{9,8},{10,11... | collective-permute-start | bytes 3538952 | tf_op jit(solution)/shard_map/ppermute | solution.py:180
  102.9 25.6 %collective-permute-start.17 = (bf16[8,48,1536]{2,1,0:T(8,128)(2,1)S(1)}, bf16[8,48,1536]{2,1,0:T(8,128)(2,1)S(1)}, u32[]{:S(2)}, u32[]{:S(2)}) collective-permute-start(bf16[8,48,1536]{2,1,0:T(8,128)(2,1)S(1)} %pad_maximum_fusion.4), channel_id=1, source_target_pairs={{0,4},{2,6},{4,0},{6,2},{8,12},{10,14},{12,8},{14,10},{16,20},{18,... | collective-permute-start | bytes 3538952 | tf_op jit(solution)/shard_map/ppermute | solution.py:179
  128.0 35.1 %collective-permute-start.13 = (bf16[16,48,1536]{2,1,0:T(8,128)(2,1)}, bf16[16,48,1536]{2,1,0:T(8,128)(2,1)}, u32[]{:S(2)}, u32[]{:S(2)}) collective-permute-start(bf16[16,48,1536]{2,1,0:T(8,128)(2,1)} %get-tuple-element.133), channel_id=1, source_target_pairs={{0,2},{2,0},{4,6},{6,4},{8,10},{10,8},{12,14},{14,12},{16,18},{18,... | collective-permute-start | bytes 7077896 | tf_op jit(solution)/shard_map/ppermute | solution.py:179
  130.2 54.8 %collective-permute-start.18 = (bf16[16,48,1536]{2,1,0:T(8,128)(2,1)}, bf16[16,48,1536]{2,1,0:T(8,128)(2,1)}, u32[]{:S(2)}, u32[]{:S(2)}) collective-permute-start(bf16[16,48,1536]{2,1,0:T(8,128)(2,1)} %get-tuple-element.131), channel_id=1, source_target_pairs={{0,2},{2,0},{4,6},{6,4},{8,10},{10,8},{12,14},{14,12},{16,18},{18,... | collective-permute-start | bytes 7077896 | tf_op jit(solution)/shard_map/ppermute | solution.py:179
  162.2 52.4 %collective-permute-start.7 = (bf16[1024,1152]{1,0:T(8,128)(2,1)}, bf16[1024,1152]{1,0:T(8,128)(2,1)}, u32[]{:S(2)}, u32[]{:S(2)}) collective-permute-start(bf16[1024,1152]{1,0:T(8,128)(2,1)} %add_convert_fusion.3), channel_id=1, source_target_pairs={{0,2},{2,0},{4,6},{6,4},{8,10},{10,8},{12,14},{14,12},{16,18},{18,... | collective-permute-start | bytes 7077896 | tf_op jit(solution)/shard_map/ppermute | solution.py:179
  324.1 227.5 %collective-permute-start.19 = (bf16[1024,768]{0,1:T(8,128)(2,1)}, bf16[1024,768]{0,1:T(8,128)(2,1)}, u32[]{:S(2)}, u32[]{:S(2)}) collective-permute-start(bf16[1024,768]{0,1:T(8,128)(2,1)} %add_convert_fusion.5), channel_id=1, source_target_pairs={{0,0},{1,2},{2,1},{3,3},{4,4},{5,6},{6,5},{7,7},{8,8},{9,10},{10,9... | collective-permute-start | bytes 4718600 | tf_op jit(solution)/shard_map/ppermute | solution.py:330
  337.3 37.7 %collective-permute-start.21 = (bf16[1024,384]{1,0:T(8,128)(2,1)}, bf16[1024,384]{1,0:T(8,128)(2,1)}, u32[]{:S(2)}, u32[]{:S(2)}) collective-permute-start(bf16[1024,384]{1,0:T(8,128)(2,1)} %convolution_convert_fusion.6), channel_id=1, source_target_pairs={{0,2},{2,0},{4,6},{6,4},{8,10},{10,8},{12,14},{14,12},{16,18},{18,... | collective-permute-start | bytes 2359304 | tf_op jit(solution)/shard_map/ppermute | solution.py:179
  368.4 169.8 %collective-permute-start.29 = (bf16[16,48,1536]{2,1,0:T(8,128)(2,1)}, bf16[16,48,1536]{2,1,0:T(8,128)(2,1)}, u32[]{:S(2)}, u32[]{:S(2)}) collective-permute-start(bf16[16,48,1536]{2,1,0:T(8,128)(2,1)} %slice.322), channel_id=1, source_target_pairs={{0,2},{2,0},{4,6},{6,4},{8,10},{10,8},{12,14},{14,12},{16,18},{18,... | collective-permute-start | bytes 7077896 | tf_op jit(solution)/shard_map/ppermute | solution.py:179
  425.3 39.9 %collective-permute-start.22 = (bf16[1024,1152]{1,0:T(8,128)(2,1)}, bf16[1024,1152]{1,0:T(8,128)(2,1)}, u32[]{:S(2)}, u32[]{:S(2)}) collective-permute-start(bf16[1024,1152]{1,0:T(8,128)(2,1)} %get-tuple-element.23), channel_id=1, source_target_pairs={{0,2},{2,0},{4,6},{6,4},{8,10},{10,8},{12,14},{14,12},{16,18},{18,... | collective-permute-start | bytes 7077896 | tf_op jit(solution)/shard_map/ppermute | solution.py:179
  455.1 90.2 %collective-permute-start.34 = (bf16[16,48,1536]{2,1,0:T(8,128)(2,1)}, bf16[16,48,1536]{2,1,0:T(8,128)(2,1)}, u32[]{:S(2)}, u32[]{:S(2)}) collective-permute-start(bf16[16,48,1536]{2,1,0:T(8,128)(2,1)} %slice.333), channel_id=1, source_target_pairs={{0,2},{2,0},{4,6},{6,4},{8,10},{10,8},{12,14},{14,12},{16,18},{18,... | collective-permute-start | bytes 7077896 | tf_op jit(solution)/shard_map/ppermute | solution.py:179
  538.1 44.2 %collective-permute-start.24 = (bf16[16,48,1664]{2,1,0:T(8,128)(2,1)}, bf16[16,48,1664]{2,1,0:T(8,128)(2,1)}, u32[]{:S(2)}, u32[]{:S(2)}) collective-permute-start(bf16[16,48,1664]{2,1,0:T(8,128)(2,1)} %slice.304), channel_id=1, source_target_pairs={{0,2},{2,0},{4,6},{6,4},{8,10},{10,8},{12,14},{14,12},{16,18},{18,... | collective-permute-start | bytes 7667720 | tf_op jit(solution)/shard_map/ppermute | solution.py:179
  542.5 29.4 %collective-permute-start.30 = (bf16[8,48,1536]{2,1,0:T(8,128)(2,1)}, bf16[8,48,1536]{2,1,0:T(8,128)(2,1)}, u32[]{:S(2)}, u32[]{:S(2)}) collective-permute-start(bf16[8,48,1536]{2,1,0:T(8,128)(2,1)} %slice.324), channel_id=1, source_target_pairs={{0,1},{1,0},{2,3},{3,2},{4,5},{5,4},{6,7},{7,6},{8,9},{9,8},{10,11... | collective-permute-start | bytes 3538952 | tf_op jit(solution)/shard_map/ppermute | solution.py:180
  549.6 28.9 %collective-permute-start.35 = (bf16[8,48,1536]{2,1,0:T(8,128)(2,1)}, bf16[8,48,1536]{2,1,0:T(8,128)(2,1)}, u32[]{:S(2)}, u32[]{:S(2)}) collective-permute-start(bf16[8,48,1536]{2,1,0:T(8,128)(2,1)} %slice.335), channel_id=1, source_target_pairs={{0,4},{2,6},{4,0},{6,2},{8,12},{10,14},{12,8},{14,10},{16,20},{18,... | collective-permute-start | bytes 3538952 | tf_op jit(solution)/shard_map/ppermute | solution.py:179
  573.8 17.3 %collective-permute-start.31 = (bf16[4,48,1536]{2,1,0:T(8,128)(2,1)S(1)}, bf16[4,48,1536]{2,1,0:T(8,128)(2,1)S(1)}, u32[]{:S(2)}, u32[]{:S(2)}) collective-permute-start(bf16[4,48,1536]{2,1,0:T(8,128)(2,1)S(1)} %slice.326), channel_id=1, source_target_pairs={{0,4},{2,6},{4,0},{6,2},{8,12},{10,14},{12,8},{14,10},{16,20},{18,... | collective-permute-start | bytes 1769480 | tf_op jit(solution)/shard_map/ppermute | solution.py:179
  580.1 16.5 %collective-permute-start.36 = (bf16[4,48,1536]{2,1,0:T(8,128)(2,1)S(1)}, bf16[4,48,1536]{2,1,0:T(8,128)(2,1)S(1)}, u32[]{:S(2)}, u32[]{:S(2)}) collective-permute-start(bf16[4,48,1536]{2,1,0:T(8,128)(2,1)S(1)} %slice.337), channel_id=1, source_target_pairs={{0,1},{1,0},{2,3},{3,2},{4,5},{5,4},{6,7},{7,6},{8,9},{9,8},{10,11... | collective-permute-start | bytes 1769480 | tf_op jit(solution)/shard_map/ppermute | solution.py:180
  585.7 37.8 %collective-permute-start.25 = (bf16[8,48,1664]{2,1,0:T(8,128)(2,1)S(1)}, bf16[8,48,1664]{2,1,0:T(8,128)(2,1)S(1)}, u32[]{:S(2)}, u32[]{:S(2)}) collective-permute-start(bf16[8,48,1664]{2,1,0:T(8,128)(2,1)S(1)} %slice.306), channel_id=1, source_target_pairs={{0,1},{1,0},{2,3},{3,2},{4,5},{5,4},{6,7},{7,6},{8,9},{9,8},{10,11... | collective-permute-start | bytes 3833864 | tf_op jit(solution)/shard_map/ppermute | solution.py:180
  588.1 58.2 %collective-permute-start.23 = (bf16[1024,768]{0,1:T(8,128)(2,1)S(1)}, bf16[1024,768]{0,1:T(8,128)(2,1)S(1)}, u32[]{:S(2)}, u32[]{:S(2)}) collective-permute-start(bf16[1024,768]{0,1:T(8,128)(2,1)S(1)} %fusion.26), channel_id=1, source_target_pairs={{0,0},{1,2},{2,1},{3,3},{4,4},{5,6},{6,5},{7,7},{8,8},{9,10},{10,9... | collective-permute-start | bytes 4718600 | tf_op jit(solution)/shard_map/ppermute | solution.py:351
  591.3 34.7 %collective-permute-start.32 = (bf16[2,48,1536]{2,1,0:T(8,128)(2,1)S(1)}, bf16[2,48,1536]{2,1,0:T(8,128)(2,1)S(1)}, u32[]{:S(2)}, u32[]{:S(2)}) collective-permute-start(bf16[2,48,1536]{2,1,0:T(8,128)(2,1)S(1)} %slice.328), channel_id=1, source_target_pairs={{0,8},{2,10},{4,12},{6,14},{8,0},{10,2},{12,4},{14,6},{16,24},{18,... | collective-permute-start | bytes 884744 | tf_op jit(solution)/shard_map/ppermute | solution.py:179
  596.7 29.5 %collective-permute-start.37 = (bf16[2,48,1536]{2,1,0:T(8,128)(2,1)S(1)}, bf16[2,48,1536]{2,1,0:T(8,128)(2,1)S(1)}, u32[]{:S(2)}, u32[]{:S(2)}) collective-permute-start(bf16[2,48,1536]{2,1,0:T(8,128)(2,1)S(1)} %slice.339), channel_id=1, source_target_pairs={{0,8},{2,10},{4,12},{6,14},{8,0},{10,2},{12,4},{14,6},{16,24},{18,... | collective-permute-start | bytes 884744 | tf_op jit(solution)/shard_map/ppermute | solution.py:179
  623.9 14.1 %collective-permute-start.26 = (bf16[4,48,1664]{2,1,0:T(8,128)(2,1)S(1)}, bf16[4,48,1664]{2,1,0:T(8,128)(2,1)S(1)}, u32[]{:S(2)}, u32[]{:S(2)}) collective-permute-start(bf16[4,48,1664]{2,1,0:T(8,128)(2,1)S(1)} %slice.308), channel_id=1, source_target_pairs={{0,4},{2,6},{4,0},{6,2},{8,12},{10,14},{12,8},{14,10},{16,20},{18,... | collective-permute-start | bytes 1916936 | tf_op jit(solution)/shard_map/ppermute | solution.py:179
  626.3 19.2 %collective-permute-start.38 = (bf16[1,48,1536]{2,1,0:T(8,128)(2,1)S(1)}, bf16[1,48,1536]{2,1,0:T(8,128)(2,1)S(1)}, u32[]{:S(2)}, u32[]{:S(2)}) collective-permute-start(bf16[1,48,1536]{2,1,0:T(8,128)(2,1)S(1)} %slice.341), channel_id=1, source_target_pairs={{0,16},{2,18},{4,20},{6,22},{8,24},{10,26},{12,28},{14,30},{16,0},... | collective-permute-start | bytes 442376 | tf_op jit(solution)/shard_map/ppermute | solution.py:179
  (63 other events, 1188.9 us)

commit v2 on v1

--- a/solution.py
+++ b/solution.py
@@ -18,6 +18,10 @@
 NT = (((1,), (1,)), ((), ()))
 TN = (((0,), (0,)), ((), ()))
 BOTH = ("dp", "tensor")
+MESH_ID = pl.DeviceIdType.MESH
+ANY = pl.BlockSpec(memory_space=pl.ANY)
+VM = pl.BlockSpec(memory_space=pltpu.VMEM)
+SM = pl.BlockSpec(memory_space=pltpu.SMEM)
 
 
 def attn_info(seg, core):
@@ -80,8 +84,6 @@
     okeep[...]=osc[pl.ds(pl.multiple_of(c*half,half),half)]
     osend[...]=osc[pl.ds(pl.multiple_of((1-c)*half,half),half)]
 
-VM=pl.BlockSpec(memory_space=pltpu.VMEM)
-SM=pl.BlockSpec(memory_space=pltpu.SMEM)
 def attn_fwd(own,recv,starts,info):
     half,cols=own.shape[0],own.shape[1]//3; n=2*half
     return pl.pallas_call(fwd_kernel,
@@ -169,63 +171,175 @@
     return lax.dot_general(left, right, dims, preferred_element_type=f32)
 
 
-def phase_order(dp_size, last):
-    high = [1 << k for k in range(dp_size.bit_length() - 2, 1, -1)]
-    return high + ([2, 0, 1] if last == "tensor" else [0, 2, 1]) if dp_size > 2 else [0, 1]
-
-
 def exchange(value, bit, dp_size):
     if bit:
         return lax.ppermute(value, "dp", [(i, i ^ bit) for i in range(dp_size)])
     return lax.ppermute(value, "tensor", [(0, 1), (1, 0)])
 
 
-def gather_blocks(shard, order, dp_size):
-    held = shard[None]
-    for bit in order:
-        held = jnp.concatenate([held, exchange(held, bit, dp_size)], axis=0)
-    return held
-
-
-def scatter_sum(partial, order, dp_size):
-    kept = partial
-    for bit in reversed(order):
-        n = kept.shape[0] // 2
-        got = exchange(kept[n:], bit, dp_size)
-        kept = (kept[:n].astype(f32) + got.astype(f32)).astype(bf)
-    return kept[0]
-
-
-def positions(order, dp_size, dp_pos, tensor_pos):
-    d = jnp.arange(dp_size, dtype=jnp.int32) ^ dp_pos
-    out = []
-    for t in range(2):
-        place = jnp.zeros((dp_size,), jnp.int32)
-        for k, bit in enumerate(order):
-            on = ((d & bit) != 0).astype(jnp.int32) if bit else (tensor_pos != t).astype(jnp.int32)
-            place = place + (on << k)
-        out.append(place)
-    return jnp.concatenate(out)
-
-
-def move_kernel(table, source, out):
-    out[...] = source[...]
-
-
-def move_blocks(blocks, table, scatter):
-    count, rows, cols = blocks.shape
-    one, other = (lambda g, s: (g, 0, 0)), (lambda g, s: (s[g], 0, 0))
+def flip(index, bits):
+    for bit in bits:
+        index = index + bit * (1 - 2 * ((index // bit) % 2))
+    return index
+
+def far_groups(dp_size):
+    far = [1 << k for k in range(dp_size.bit_length() - 2, 1, -1)]
+    return [tuple(far[k : k + 2]) for k in range(0, len(far), 2)]
+
+def group_moves(group):
+    if len(group) == 1:
+        return [(1, group)]
+    return [(1, group[:1]), (2, group[1:]), (3, group)]
+
+def chunks_of(cols, which, count, until=None):
+    tiles = cols // 128
+    cuts = [128 * ((tiles * k) // count) for k in range(count + 1)]
+    arrays = range(which, until + 1) if until else (which,)
+    return tuple(
+        (array, low, high - low, 128 * max(1, (high - low) * 2 // 3 // 128))
+        for low, high in zip(cuts, cuts[1:]) for array in arrays)
+
+
+def head_kernel(groups, chunks, tokens, *refs):
+    shards, x_out, outs, (send_sem, recv_sem, local_sem) = refs[:4], refs[4], refs[5:9], refs[9:]
+    dp, t = lax.axis_index("dp"), lax.axis_index("tensor")
+    core = dp % 2
+    away = core + t - 2 * core * t
+    near = {1: (flip(dp, (1,)), t), 2: (flip(dp, (2,)), t), 0: (dp, 1 - t)}
+    distant = [bits for group in groups for _, bits in group_moves(group)]
+    swap = (dp - core + t, core)
+    barrier = pltpu.get_barrier_semaphore()
+    for device in list(near.values()) + [(flip(dp, bits), t) for bits in distant]:
+        pl.semaphore_signal(barrier, inc=1, device_id=device, device_id_type=MESH_ID)
+
+    @pl.when(away == 1)
+    def _():
+        pl.semaphore_signal(barrier, inc=1, device_id=swap, device_id_type=MESH_ID)
+
+    local = [
+        pltpu.make_async_copy(shards[k], outs[k].at[away if k < 2 else 0, 0], local_sem.at[k]) for k in range(4)]
+    for copy in local:
+        copy.start()
+    pl.semaphore_wait(barrier, len(near) + len(distant) + away)
+    count = [0]
+
+    def remote(src, dst, device):
+        slot = count[0]
+        count[0] += 1
+        return pltpu.make_async_remote_copy(
+            src_ref=src, dst_ref=dst, send_sem=send_sem.at[slot], recv_sem=recv_sem.at[slot],
+            device_id=device, device_id_type=MESH_ID)
+
+    def blocks(ref, index, first, held, low, size):
+        return ref.at[index, pl.ds(first, held), :, pl.ds(low, size)]
+
+    plans = []
+    for which, low, size, half in chunks:
+        shard, out, by_group = shards[which], outs[which], which < 2
+        first = away if by_group else 0
+        steps, held = [], 1
+        for group in groups:
+            moves = []
+            for place, bits in group_moves(group):
+                src = shard.at[:, pl.ds(low, size)] if held == 1 else blocks(out, first, 0, held, low, size)
+                dst = out.at[first, place, :, pl.ds(low, size)] if held == 1 else blocks(out, first, place * held, held, low, size)
+                moves.append(remote(src, dst, (flip(dp, bits), t)))
+            held *= len(group_moves(group)) + 1
+            steps.append(moves)
+        a, b = (low, half), (low + half, size - half)
+        other = first if by_group else 1
+        steps.append([
+            remote(blocks(out, first, 0, held, *a), blocks(out, other, 0, held, *a), near[0]),
+            remote(blocks(out, first, 0, held, *b), blocks(out, first, held, held, *b), near[2]),
+        ])
+        steps.append(
+            [remote(blocks(out, k, 0, held, *a), blocks(out, k, held, held, *a), near[2]) for k in range(2)]
+            + [remote(blocks(out, first, 0, 2 * held, *b), blocks(out, other, 0, 2 * held, *b), near[0])])
+        steps.append([
+            remote(blocks(out, k, 0, 2 * held, low, size),
+                   blocks(out, 1 - k if by_group else k, 2 * held, 2 * held, low, size), near[1]) for k in range(2)])
+        plans.append(steps)
+    depth = len(plans[0])
+    swap_copy = remote(tokens, x_out, swap)
+    stay_copy = pltpu.make_async_copy(tokens, x_out, local_sem.at[4])
+    waited = set()
+
+    def advance(number, phase):
+        if number >= len(plans):
+            return
+        if phase > 0:
+            for move in plans[number][phase - 1]:
+                move.wait_recv()
+        if phase == 1 and chunks[number][0] not in waited:
+            waited.add(chunks[number][0])
+            local[chunks[number][0]].wait()
+        if phase < depth:
+            for move in plans[number][phase]:
+                move.start()
+
+    advance(0, 0)
+
+    @pl.when(away == 1)
+    def _():
+        swap_copy.start()
+
+    @pl.when(away == 0)
+    def _():
+        stay_copy.start()
+
+    far = len(groups)
+    for number in range(len(plans)):
+        if number == 0:
+            for phase in range(1, far + 1):
+                advance(0, phase)
+            advance(1, 0)
+        advance(number, far + 1)
+        for phase in range(1, far + 1):
+            advance(number + 1, phase)
+        advance(number + 2, 0)
+        advance(number, far + 2)
+    for number in range(len(plans)):
+        advance(number, depth)
+
+    @pl.when(away == 1)
+    def _():
+        swap_copy.wait()
+
+    @pl.when(away == 0)
+    def _():
+        stay_copy.wait()
+
+    for which in sorted(set(range(4)) - waited):
+        local[which].wait()
+    for steps in plans:
+        for moves in steps:
+            for move in moves:
+                move.wait_send()
+
+
+def head(dp_size, tokens, shards, chunks):
+    groups = far_groups(dp_size)
+    slots = len(chunks) * (sum(len(group_moves(g)) for g in groups) + 7) + 1
     return pl.pallas_call(
-        move_kernel,
-        grid_spec=pltpu.PrefetchScalarGridSpec(
-            num_scalar_prefetch=1,
-            grid=(count,),
-            in_specs=[pl.BlockSpec((1, rows, cols), one if scatter else other)],
-            out_specs=pl.BlockSpec((1, rows, cols), other if scatter else one),
-        ),
-        out_shape=jax.ShapeDtypeStruct(blocks.shape, blocks.dtype),
-        cost_estimate=pl.CostEstimate(flops=0, bytes_accessed=4 * blocks.size, transcendentals=0),
-    )(table, blocks)
+        functools.partial(head_kernel, groups, chunks),
+        in_specs=[VM] * 5,
+        out_specs=[ANY] * 5,
+        out_shape=[jax.ShapeDtypeStruct(tokens.shape, tokens.dtype)]
+        + [jax.ShapeDtypeStruct((2, dp_size) + s.shape, s.dtype) for s in shards],
+        scratch_shapes=[pltpu.SemaphoreType.DMA((slots,)), pltpu.SemaphoreType.DMA((slots,)), pltpu.SemaphoreType.DMA((5,))],
+        compiler_params=pltpu.CompilerParams(collective_id=0, has_side_effects=True),
+    )(tokens, *shards)
+
+
+def halve_rows(kept, bits, dp_size):
+    for bit in bits:
+        n = kept[0].shape[0] // 2
+        kept = [add_low(k[:n], exchange(k[n:], bit, dp_size)) for k in kept]
+    return kept
+
+
+def add_low(left, right):
+    return (left.astype(f32) + right.astype(f32)).astype(bf)
 
 
 def layer_norm_parts(values):
@@ -266,71 +380,90 @@
     cols = w_qkv.shape[2]
     hidden = w_fc.shape[1]
     fan = b_fc.shape[0] // rows
-    first, second = phase_order(dp_size, "tensor"), phase_order(dp_size, "x")
+    far = [1 << k for k in range(dp_size.bit_length() - 2, 1, -1)]
     swap = []
     for d in range(dp_size):
         for t in range(2):
             swap.append((2 * d + t, 2 * (d - d % 2 + t) + d % 2))
     mine = core == t_pos
 
-    residual_in = lax.ppermute(tokens, BOTH, swap)
-    seg_other = lax.ppermute(segment_ids, "dp", [(i, i ^ 1) for i in range(dp_size)])
+    seg_other = exchange(segment_ids, 1, dp_size)
     seg = jnp.where(mine, segment_ids, seg_other)[0]
     small = jnp.concatenate(
         [ln1_gain[:, None], ln1_bias[:, None], b_qv.T, b_attn_out[:, None], ln2_gain[:, None],
          ln2_bias[:, None], b_proj[:, None], b_fc.reshape(rows, fan)], axis=1)
     small = jnp.pad(small, ((0, 0), (0, SMALL - small.shape[1])))
-    pack_a = jnp.concatenate([w_qkv.reshape(rows, 3 * cols), w_attn_out.T, small], axis=1)
-    place_a = positions(first, dp_size, dp_pos, t_pos)
-    place_b = positions(second, dp_size, dp_pos, t_pos)
-    all_a = move_blocks(gather_blocks(pack_a, first, dp_size), place_a, False).reshape(2, width, -1)
-    all_fc = move_blocks(gather_blocks(w_fc, first, dp_size), place_a, False).reshape(2, width, hidden)
-    all_proj = move_blocks(gather_blocks(w_proj.T, second, dp_size), place_b, False).reshape(2, width, hidden)
-    qkv_w = all_a[:, :, : 3 * cols]
-    out_w = all_a[:, :, 3 * cols : 4 * cols]
-    vec = all_a[0, :, 4 * cols :].astype(f32).T
-    gain1, bias1, b_q, b_v, out_bias, gain2, bias2, proj_bias = (vec[k] for k in range(8))
-    fc_bias = vec[8 : 8 + fan].T.reshape(2, hidden)
-    qkv_bias = jnp.stack([b_q.reshape(2, cols), jnp.zeros((2, cols), f32), b_v.reshape(2, cols)], axis=1).reshape(2, 3 * cols)
-
-    x = residual_in.astype(f32)
+    out_pack = jnp.concatenate([w_attn_out.T, small], axis=1)
+    tokens, all_qkv, all_out, all_fc, all_proj = head(
+        dp_size, tokens, (w_qkv.reshape(rows, 3 * cols), out_pack, w_fc, w_proj.T),
+        chunks_of(3 * cols, 0, 2) + chunks_of(cols + SMALL, 1, 1) + chunks_of(hidden, 2, 2, 3))
+    all_qkv, all_out, all_fc, all_proj = (a.reshape(2, width, -1) for a in (all_qkv, all_out, all_fc, all_proj))
+
+    place = jnp.arange(width, dtype=jnp.int32)
+    block = place // rows
+    source = jnp.zeros_like(block)
+    for k, bit in enumerate(far + [2, 1]):
+        source = source + ((block >> k) & 1) * bit
+    natural = (source ^ dp_pos) * rows + place % rows
+    order = (place[:, None] == natural[None, :]).astype(bf)
+
+    vec_rel = all_out[0, :, cols:]
+    vec_nat = dot(order, vec_rel).T
+    vec_rel = vec_rel.astype(f32).T
+    gain1, bias1, _, _, out_bias, gain2, bias2, proj_bias = (vec_rel[k] for k in range(8))
+    fc_bias = vec_nat[8 : 8 + fan].T.reshape(2, hidden)
+    b_q, b_v = vec_nat[2].reshape(2, cols), vec_nat[3].reshape(2, cols)
+    take = lambda arr, k: lax.dynamic_index_in_dim(arr, k, 0, keepdims=False)
+    other = 1 - core
+    qkv_bias = lambda k: jnp.concatenate([take(b_q, k), jnp.zeros((cols,), f32), take(b_v, k)])
+
+    x = dot(tokens, order)
     hat1, inv1 = layer_norm_parts(x)
     n1 = (hat1 * gain1 + bias1).astype(bf)
-    take = lambda arr, k: lax.dynamic_index_in_dim(arr, k, 0, keepdims=False)
-    other = 1 - core
-    qkv_send = (dot(n1, take(qkv_w, other)) + take(qkv_bias, other)).astype(bf)
+    wq_own, wq_other = all_qkv[0], all_qkv[1]
+    wo_own, wo_other = all_out[0, :, :cols], all_out[1, :, :cols]
+    qkv_send = (dot(n1, wq_other) + qkv_bias(other)).astype(bf)
     qkv_recv = exchange(qkv_send, 1, dp_size)
-    qkv_own = (dot(n1, take(qkv_w, core)) + take(qkv_bias, core)).astype(bf)
+    qkv_own = (dot(n1, wq_own) + qkv_bias(core)).astype(bf)
     starts, info = attn_info(seg, core)
     o_own, o_send, lse = attn_fwd(qkv_own, qkv_recv, starts, info)
     o_recv = exchange(o_send, 1, dp_size)
-    wo_own, wo_other = take(out_w, core), take(out_w, other)
     branch = dot(o_own, wo_own, NT) + dot(o_recv, wo_other, NT) + out_bias
     middle = x + BRANCH_SCALE * branch
     hat2, inv2 = layer_norm_parts(middle)
     n2 = (hat2 * gain2 + bias2).astype(bf)
-    grad_out = lax.ppermute(cotangent, BOTH, swap).astype(f32)
+    grad_out = dot(lax.ppermute(cotangent, BOTH, swap), order)
     scaled_out = BRANCH_SCALE * grad_out
     d_b_proj = jnp.sum(scaled_out, axis=0)
     d_mlp = scaled_out.astype(bf)
     mlp = jnp.zeros_like(x)
     d_n2 = jnp.zeros_like(x)
-    d_fc, d_proj, d_b_fc = [], [], []
-    for t in range(2):
-        act, slope = gelu_parts(dot(n2, all_fc[t]) + fc_bias[t])
+    half = width // 2
+
+    def weight_grad(left, right):
+        return dot(left[:, :half], right, TN).astype(bf), dot(left[:, half:], right, TN).astype(bf)
+
+    sum_fc, sum_proj, d_b_fc = [], [], []
+    for k in range(2):
+        act, slope = gelu_parts(dot(n2, all_fc[k]) + take(fc_bias, t_pos ^ k))
         act = act.astype(bf)
-        mlp = mlp + dot(act, all_proj[t], NT)
-        d_pre = dot(d_mlp, all_proj[t]) * slope
+        mlp = mlp + dot(act, all_proj[k], NT)
+        d_pre = dot(d_mlp, all_proj[k]) * slope
         d_b_fc.append(jnp.sum(d_pre, axis=0))
         d_pre = d_pre.astype(bf)
-        d_n2 = d_n2 + dot(d_pre, all_fc[t], NT)
-        d_fc.append(dot(n2, d_pre, TN).astype(bf))
-        d_proj.append(dot(d_mlp, act, TN).astype(bf))
+        d_n2 = d_n2 + dot(d_pre, all_fc[k], NT)
+        keep, send = weight_grad(n2, d_pre)
+        sum_fc.append(add_low(keep, exchange(send, 1, dp_size)))
+        keep, send = weight_grad(d_mlp, act)
+        sum_proj.append(add_low(keep, exchange(send, 1, dp_size)))
+    down = far[::-1]
+    sum_fc = add_low(sum_fc[0], exchange(sum_fc[1], 0, dp_size))
+    (sum_fc,) = halve_rows([sum_fc], [2] + down, dp_size)
+    sum_proj = halve_rows(sum_proj, [2], dp_size)
+    sum_proj = add_low(sum_proj[0], exchange(sum_proj[1], 0, dp_size))
+    (sum_proj,) = halve_rows([sum_proj], down, dp_size)
     block_out = (middle + BRANCH_SCALE * (mlp + proj_bias)).astype(bf)
-    block_out = lax.ppermute(block_out, BOTH, swap)
-    blocks = lambda parts: jnp.stack(parts).reshape(2 * dp_size, rows, -1)
-    sum_fc = scatter_sum(move_blocks(blocks(d_fc), place_a, True), first, dp_size)
-    sum_proj = scatter_sum(move_blocks(blocks(d_proj), place_b, True), second, dp_size)
+    block_out = lax.ppermute(dot(block_out, order, NT).astype(bf), BOTH, swap)
 
     back2, d_gain2, d_bias2 = layer_norm_back(hat2, inv2, gain2, d_n2)
     d_middle = grad_out + back2
@@ -340,27 +473,35 @@
     do_send = dot(d_attn, wo_other).astype(bf)
     do_recv = exchange(do_send, 1, dp_size)
     do_own = dot(d_attn, wo_own).astype(bf)
-    dwo_own = dot(d_attn, o_own, TN).astype(bf)
-    dwo_other = dot(d_attn, o_recv, TN).astype(bf)
+
+    def reduce_pair(own_keep, own_send, other_keep, other_send):
+        own = add_low(own_keep, exchange(other_send, 1, dp_size))
+        rest = add_low(other_keep, exchange(own_send, 1, dp_size))
+        keep, send = jnp.where(mine, own, rest), jnp.where(mine, rest, own)
+        total = add_low(keep, exchange(send, 0, dp_size))
+        (total,) = halve_rows([total], [2] + down, dp_size)
+        return total
+
+    sum_out = reduce_pair(*weight_grad(d_attn, o_own), *weight_grad(d_attn, o_recv))
     dq_own, dq_send = attn_bwd(qkv_own, qkv_recv, do_own, do_recv, o_own, o_send, starts, lse, info)
     dq_recv = exchange(dq_send, 1, dp_size)
-    d_n1 = dot(dq_own, take(qkv_w, core), NT) + dot(dq_recv, take(qkv_w, other), NT)
-    dwq_own = dot(n1, dq_own, TN).astype(bf)
-    dwq_other = dot(n1, dq_recv, TN).astype(bf)
+    d_n1 = dot(dq_own, wq_own, NT) + dot(dq_recv, wq_other, NT)
     back1, d_gain1, d_bias1 = layer_norm_back(hat1, inv1, gain1, d_n1)
-    grad_tokens = lax.ppermute((d_middle + back1).astype(bf), BOTH, swap)
+    grad_tokens = dot((d_middle + back1).astype(bf), order, NT).astype(bf)
+    grad_tokens = lax.ppermute(grad_tokens, BOTH, swap)
     s_own = jnp.sum(dq_own.astype(f32), axis=0).reshape(3, cols)
     s_other = jnp.sum(dq_recv.astype(f32), axis=0).reshape(3, cols)
-    pick = lambda a, b: jnp.where(core == 0, jnp.concatenate([a, b]), jnp.concatenate([b, a]))
-    d_small = jnp.stack(
-        [d_gain1, d_bias1, pick(s_own[0], s_other[0]), pick(s_own[2], s_other[2]), d_b_out, d_gain2, d_bias2, d_b_proj], axis=1)
-    d_small = jnp.concatenate(
-        [d_small, jnp.concatenate(d_b_fc).reshape(width, fan), jnp.zeros((width, SMALL - 8 - fan), f32)], axis=1).astype(bf)
-    own_a = jnp.concatenate([dwq_own, dwo_own, d_small], axis=1)
-    other_a = jnp.concatenate([dwq_other, dwo_other, d_small], axis=1)
-    part_a = jnp.where(core == 0, jnp.stack([own_a, other_a]), jnp.stack([other_a, own_a])).reshape(2 * dp_size, rows, -1)
-    sum_a = scatter_sum(move_blocks(part_a, place_a, True), first, dp_size).astype(f32)
-    vecs = sum_a[:, 4 * cols :]
+    pick = lambda cond, a, b: jnp.where(cond, jnp.concatenate([a, b]), jnp.concatenate([b, a]))
+    nat = jnp.concatenate(
+        [pick(core == 0, s_own[0], s_other[0])[:, None], pick(core == 0, s_own[2], s_other[2])[:, None],
+         pick(t_pos == 0, *d_b_fc).reshape(width, fan)], axis=1).astype(bf)
+    nat = dot(order, nat, TN)
+    d_small = jnp.stack([d_gain1, d_bias1, nat[:, 0], nat[:, 1], d_b_out, d_gain2, d_bias2, d_b_proj], axis=1)
+    d_small = jnp.concatenate([d_small, nat[:, 2:], jnp.zeros((width, SMALL - 8 - fan), f32)], axis=1).astype(bf)
+    with_small = lambda pair: [
+        jnp.concatenate([pair[0], d_small[:half]], axis=1), jnp.concatenate([pair[1], d_small[half:]], axis=1)]
+    sum_a = reduce_pair(*with_small(weight_grad(n1, dq_own)), *with_small(weight_grad(n1, dq_recv))).astype(f32)
+    vecs = sum_a[:, 3 * cols :]
     return (
         block_out,
         grad_tokens,
@@ -368,7 +509,7 @@
         vecs[:, 1],
         sum_a[:, : 3 * cols].reshape(rows, 3, cols),
         vecs[:, 2:4].T,
-        sum_a[:, 3 * cols : 4 * cols].T,
+        sum_out.astype(f32).T,
         vecs[:, 4],
         vecs[:, 5],
         vecs[:, 6],

time: 667 us -> 487 us (0.73)
  waiting for transfers between devices: 141 us -> 64 us
  local copies, waits for them, and re-layouts: 100 us -> 46.8 us
  other arithmetic: 48.5 us -> 16.5 us
  starting transfers between devices: 62.8 us -> 40.1 us
  matrix products: 94.8 us -> 115 us
  Pallas kernels: 208 us -> 195 us
    ppermute x6 -> x4, waiting for transfers between devices: 104 us -> 20.6 us  [exchange(): return lax.ppermute(value, 'tensor', [(0, 1), (1, 0)])]
    concatenate x13 -> x1, local copies, waits for them, and re-layouts: 28.2 us -> 2.65 us  [on_device(): jnp.concatenate([d_small, nat[:, 2:], jnp.zeros((width, SMALL - 8 - fan),...]
    dot_general x24 -> x37, matrix products: 94.8 us -> 115 us  [dot(): return lax.dot_general(left, right, dims, preferred_element_type=f32)]
    slice x26 -> x22, local copies, waits for them, and re-layouts: 29.7 us -> 13.8 us  [the longest x1 7.74 us: on_device(): mlp = mlp + dot(act, all_proj[k], NT)]
    ppermute x5 -> x3, starting transfers between devices: 29.3 us -> 16.4 us  [the longest x1 13.5 us: on_device(): grad_out = dot(lax.ppermute(cotangent, BOTH, swap), order)]
    pallas_call x6 -> x1, Pallas kernels: 113 us -> 102 us  [head(): pl.pallas_call(functools.partial(head_kernel, groups, chunks), in_specs=[...]
    another operation x5 -> x3, other arithmetic: 10.9 us -> 0.03 us  [the longest x2 7.56 us: on_device(): blocks = lambda parts: jnp.stack(parts).reshape(2 * dp_size, rows, -1)]
    unnamed x131 -> x121, local copies, waits for them, and re-layouts: 23.5 us -> 14.6 us
  transfers between devices with their start and end apart: 39 -> 33, of which waited for: 14 -> 12; matrix products, arithmetic and copies ran while one was open for 28% -> 19% of each run, Pallas kernels for 32% -> 20%
where the time goes in v2:
time: 487 us; the launch traced here: 479 us
  Pallas kernels  195 us (40%)
  matrix products  115 us (24%)
  waiting for transfers between devices  64 us (13%)
  local copies, waits for them, and re-layouts  46.8 us (10%)
  starting transfers between devices  40.1 us (8%)
  other arithmetic  16.5 us (3%)
    dot_general x37, matrix products, dot(): return lax.dot_general(left, right, dims, preferred_element_type=f32)  115 us
    pallas_call x1, Pallas kernels, head(): pl.pallas_call(functools.partial(head_kernel, groups, chunks), in_specs=[...  102 us
    pallas_call x1, Pallas kernels, attn_bwd(): pl.pallas_call(bwd_kernel, in_specs=[SM] + [VM] * 8, out_specs=[VM] * 2,...  50.3 us
    ppermute x26, waiting for transfers between devices, exchange(): return lax.ppermute(value, 'dp', [(i, i ^ bit) for i in range(dp_size)])  43.3 us
    pallas_call x1, Pallas kernels, attn_fwd(): pl.pallas_call(fwd_kernel, in_specs=[SM, VM, VM, VM], out_specs=[VM] * 3,...  43.2 us
    ppermute x4, waiting for transfers between devices, exchange(): return lax.ppermute(value, 'tensor', [(0, 1), (1, 0)])  20.6 us
    ppermute x26, starting transfers between devices, exchange(): return lax.ppermute(value, 'dp', [(i, i ^ bit) for i in range(dp_size)])  17.8 us
    unnamed x121, local copies, waits for them, and re-layouts  14.6 us
  transfers between devices with their start and end apart: 33, of which 12 were waited for; matrix products, arithmetic and copies ran while one was open for 19% of the time, Pallas kernels for 20%

profile of v2, /device:TPU:0, one launch (start us, length us, event | category | flops | bytes accessed | tf_op | source)
XLA Modules:
  0.0 479.3 jit_solution(6429446429450631681)
XLA Ops:
  9.8 101.6 %shard_map.254 = (bf16[1024,768]{1,0:T(8,128)(2,1)}, bf16[2,16,48,1152]{3,2,1,0:T(8,128)(2,1)}, bf16[2,16,48,512]{3,2,1,0:T(8,128)(2,1)}, bf16[2,16,48,1536]{3,2,1,0:T(8,128)(2,1)}, bf16[2,16,48,1536]{3,2,1,0:T(8,128)(2,1)}) custom-call(bf16[1024,768]{1,0:T(8,128)(2,1)} %tokens.1, bf16[48,1152]{1,0:T(8,128)(2,1)} %bitcast.127, ...), custom_call_target="tpu_custom_call" | custom-call | tf_op jit(solution)/shard_map/pallas_call | solution.py:323
  114.9 3.0 fusion.112
  122.1 3.8 add_convert_fusion
  126.4 13.5 %collective-permute-start.4 = (bf16[1024,768]{1,0:T(8,128)(2,1)}, bf16[1024,768]{1,0:T(8,128)(2,1)}, u32[]{:S(2)}, u32[]{:S(2)}) collective-permute-start(bf16[1024,768]{1,0:T(8,128)(2,1)} %param.29), channel_id=1, source_target_pairs={{0,0},{1,2},{2,1},{3,3},{4,4},{5,6},{6,5},{7,7},{8,8},{9,10},{10,9... | collective-permute-start | bytes 4718600 | tf_op jit(solution)/shard_map/ppermute | solution.py:435
  140.0 3.7 add_convert_fusion.1.own
  145.9 43.2 %shard_map.255 = (bf16[1024,384]{1,0:T(8,128)(2,1)S(1)}, bf16[1024,384]{1,0:T(8,128)(2,1)S(1)}, f32[6,2048]{1,0:T(8,128)S(1)}) custom-call(s32[17]{0:T(128)S(1)} %pad_add_fusion.info, bf16[1024,1152]{1,0:T(8,128)(2,1)S(1)} %copy-done.4, bf16[1024,1152]{1,0:T(8,128)(2,1)} %collective-permute-done.1.recv, s32[1,2048]{1,0:T(1,128)S(1)} %bitcast.105), custom_call_target="tpu_custom_call" | custom-call | flops 2147483520 | bytes 6291456 | tf_op jit(solution)/shard_map/pallas_call | solution.py:89
  189.8 7.7 %fusion.106 = (bf16[1,16,48,1536]{3,2,1,0:T(8,128)(2,1)}, bf16[1,16,48,1536]{3,2,1,0:T(8,128)(2,1)}, bf16[1,16,48,1536]{3,2,1,0:T(8,128)(2,1)}, bf16[1,16,48,1536]{3,2,1,0:T(8,128)(2,1)}) fusion(bf16[2,16,48,1536]{3,2,1,0:T(8,128)(2,1)} %get-tuple-element.30, bf16[2,16,48,1536]{3,2,1,0:T(8,128)(2,1)} %get-tuple-element.29), kind=kLoop, calls=%fused_computation.238 | loop fusion | bytes 18874368 | tf_op jit(solution)/shard_map/slice | solution.py:450
  198.9 3.0 fusion.13
  208.3 4.2 multiply_convert_fusion.1
  212.6 6.7 %fusion.115 = (bf16[1536]{0:T(1024)(128)(2,1)S(1)}, bf16[1024,1536]{1,0:T(8,128)(2,1)S(1)}) fusion(f32[1024,1536]{1,0:T(8,128)S(1)} %get-tuple-element.160, f32[1536]{0:T(1024)S(1)} %get-tuple-element.127, bf16[1024,768]{0,1:T(8,128)(2,1)S(1)} %get-tuple-element.163, bf16[768,1536]{1,0:T(8,128)(2,1)S(1)} %bitcast.111), kind=kOutput, calls=%fused_computation.247 | convolution fusion | flops 2448947712 | bytes 13378560 | tf_op jit(solution)/shard_map/dot_general | solution.py:171
  224.3 4.3 fusion.116
  231.0 5.9 %multiply_convert_fusion = (bf16[1024,1536]{1,0:T(8,128)(2,1)}, f32[1024,1536]{1,0:T(8,128)S(1)}) fusion(f32[1536]{0:T(1024)S(1)} %get-tuple-element.126, bf16[1024,768]{0,1:T(8,128)(2,1)S(1)} %add_convert_fusion.4, bf16[768,1536]{1,0:T(8,128)(2,1)S(1)} %bitcast.109), kind=kOutput, calls=%fused_computation.16 | convolution fusion | flops 2431647744 | bytes 13375488 | tf_op jit(solution)/shard_map/dot_general | solution.py:171
  236.9 6.7 %fusion.114 = (bf16[1536]{0:T(1024)(128)(2,1)S(1)}, bf16[1024,1536]{1,0:T(8,128)(2,1)S(1)}) fusion(f32[1024,1536]{1,0:T(8,128)S(1)} %get-tuple-element.162, f32[1536]{0:T(1024)S(1)} %get-tuple-element.126, bf16[1024,768]{0,1:T(8,128)(2,1)S(1)} %get-tuple-element.163, bf16[768,1536]{1,0:T(8,128)(2,1)S(1)} %bitcast.108), kind=kOutput, calls=%fused_computation.246 | convolution fusion | flops 2448947712 | bytes 13378560 | tf_op jit(solution)/shard_map/dot_general | solution.py:171
  246.1 4.1 multiply_reduce_fusion
  259.2 9.6 %fusion.23 = bf16[1024,768]{1,0:T(8,128)(2,1)} fusion(s32[768]{0:T(1024)S(1)} %fusion.91, f32[1024,768]{0,1:T(8,128)} %copy-done.6, f32[1024,768]{0,1:T(8,128)} %fusion.116, bf16[1024,1536]{1,0:T(8,128)(2,1)} %get-tuple-element.161, bf16[768,1536]{1,0:T(8,128)(2,1)} %bitcast.107, f32[768]{0:T(1024)S(1)} %get-tuple-element.112), kind=kOutput, calls=%fused_computation.75 | convolution fusion | flops 3629187072 | bytes 13375488 | tf_op jit(solution)/shard_map/dot_general | solution.py:171
  268.8 4.8 %fusion.17 = f32[384,1536]{1,0:T(8,128)} fusion(bf16[1024,768]{0,1:T(8,128)(2,1)S(1)} %add_convert_fusion.4, bf16[1024,1536]{1,0:T(8,128)(2,1)} %copy-done.47), kind=kOutput, calls=%fused_computation.56 | convolution fusion | flops 1209139200 | bytes 6291456 | tf_op jit(solution)/shard_map/dot_general | solution.py:171
  277.3 3.4 collective-permute-start.16
  283.1 4.8 collective-permute-done.16
  288.6 3.0 convolution_convert_fusion.13.doo
  297.2 50.3 %shard_map.256 = (bf16[1024,1152]{1,0:T(8,128)(2,1)}, bf16[1024,1152]{1,0:T(8,128)(2,1)}) custom-call(s32[17]{0:T(128)} %copy-done.2, bf16[1024,1152]{1,0:T(8,128)(2,1)} %add_convert_fusion.1.own, bf16[1024,1152]{1,0:T(8,128)(2,1)} %collective-permute-done.1.recv, bf16[1024,384]{1,0:T(8,128)(2,1)} %convolution_convert_fusion.13.doo, ...), custom_call_target="tpu_custom_call" | custom-call | flops 5368709120 | bytes 12582912 | tf_op jit(solution)/shard_map/pallas_call | solution.py:160
  364.9 9.6 %collective-permute-done.29 = bf16[192,1536]{1,0:T(8,128)(2,1)S(1)} collective-permute-done((bf16[192,1536]{1,0:T(8,128)(2,1)S(1)}, bf16[192,1536]{1,0:T(8,128)(2,1)S(1)}, u32[]{:S(2)}, u32[]{:S(2)}) %collective-permute-start.29) | collective-permute-done | bytes 589856 | tf_op jit(solution)/shard_map/ppermute | solution.py:176
  377.4 3.7 add_convert_fusion.9
  382.7 7.1 %collective-permute-done.27 = bf16[192,1536]{1,0:T(8,128)(2,1)S(1)} collective-permute-done((bf16[192,1536]{1,0:T(8,128)(2,1)S(1)}, bf16[192,1536]{1,0:T(8,128)(2,1)S(1)}, u32[]{:S(2)}, u32[]{:S(2)}) %collective-permute-start.27) | collective-permute-done | bytes 589856 | tf_op jit(solution)/shard_map/ppermute | solution.py:176
  398.8 5.0 %multiply_reduce_fusion.1 = (bf16[768]{0:T(1024)(128)(2,1)S(1)}, f32[1024]{0:T(1024)}, f32[1024]{0:T(1024)}, bf16[768]{0:T(1024)(128)(2,1)S(1)}, f32[1024,768]{0,1:T(8,128)}) fusion(f32[1024,768]{0,1:T(8,128)S(1)} %copy-done.9, f32[1024]{0:T(1024)S(1)} %add_rsqrt_fusion.1, f32[1024]{0:T(1024)S(1)} %broadcast_multiply_fusion.5, ...), kind=kOutput, calls=%fused_computation.25 | convolution fusion | flops 1819800064 | bytes 13588480 | tf_op jit(solution)/shard_map/dot_general | solution.py:171
  411.9 3.2 convolution_convert_fusion.2
  425.4 4.3 collective-permute-done.32
  430.4 3.3 collective-permute-done.23
  434.9 12.4 %collective-permute-done.10 = bf16[384,1280]{1,0:T(8,128)(2,1)S(1)} collective-permute-done((bf16[384,1280]{1,0:T(8,128)(2,1)S(1)}, bf16[384,1280]{1,0:T(8,128)(2,1)S(1)}, u32[]{:S(2)}, u32[]{:S(2)}) %collective-permute-start.10) | collective-permute-done | bytes 983072 | tf_op jit(solution)/shard_map/ppermute | solution.py:177
  452.0 6.9 %collective-permute-done.11 = bf16[192,1280]{1,0:T(8,128)(2,1)S(1)} collective-permute-done((bf16[192,1280]{1,0:T(8,128)(2,1)S(1)}, bf16[192,1280]{1,0:T(8,128)(2,1)S(1)}, u32[]{:S(2)}, u32[]{:S(2)}) %collective-permute-start.11) | collective-permute-done | bytes 491552 | tf_op jit(solution)/shard_map/ppermute | solution.py:176
  460.8 5.7 %collective-permute-done.12 = bf16[96,1280]{1,0:T(8,128)(2,1)S(1)} collective-permute-done((bf16[96,1280]{1,0:T(8,128)(2,1)S(1)}, bf16[96,1280]{1,0:T(8,128)(2,1)S(1)}, u32[]{:S(2)}, u32[]{:S(2)}) %collective-permute-start.12) | collective-permute-done | bytes 245792 | tf_op jit(solution)/shard_map/ppermute | solution.py:176
  466.7 3.2 collective-permute-done.25
  470.6 3.2 collective-permute-done.13
  (304 shorter events, 122.5 us)
Async XLA Ops:
  125.9 18.3 %collective-permute-start.1 = (bf16[1024,1152]{1,0:T(8,128)(2,1)}, bf16[1024,1152]{1,0:T(8,128)(2,1)}, u32[]{:S(2)}, u32[]{:S(2)}) collective-permute-start(bf16[1024,1152]{1,0:T(8,128)(2,1)} %add_convert_fusion), channel_id=1, source_target_pairs={{0,2},{2,0},{4,6},{6,4},{8,10},{10,8},{12,14},{14,12},{16,18},{18,... | collective-permute-start | bytes 7077896 | tf_op jit(solution)/shard_map/ppermute | solution.py:176
  126.4 17.3 %collective-permute-start = (s32[1,2048]{1,0:T(1,128)S(1)}, s32[1,2048]{1,0:T(1,128)S(1)}, u32[]{:S(2)}, u32[]{:S(2)}) collective-permute-start(s32[1,2048]{1,0:T(1,128)S(1)} %copy-done.38), channel_id=1, source_target_pairs={{0,2},{2,0},{4,6},{6,4},{8,10},{10,8},{12,14},{14,12},{16,18},{18,... | collective-permute-start | bytes 24584 | tf_op jit(solution)/shard_map/ppermute | solution.py:176
  126.4 72.4 %collective-permute-start.4 = (bf16[1024,768]{1,0:T(8,128)(2,1)}, bf16[1024,768]{1,0:T(8,128)(2,1)}, u32[]{:S(2)}, u32[]{:S(2)}) collective-permute-start(bf16[1024,768]{1,0:T(8,128)(2,1)} %param.29), channel_id=1, source_target_pairs={{0,0},{1,2},{2,1},{3,3},{4,4},{5,6},{6,5},{7,7},{8,8},{9,10},{10,9... | collective-permute-start | bytes 4718600 | tf_op jit(solution)/shard_map/ppermute | solution.py:435
  189.8 12.0 %collective-permute-start.2 = (bf16[1024,384]{1,0:T(8,128)(2,1)S(1)}, bf16[1024,384]{1,0:T(8,128)(2,1)S(1)}, u32[]{:S(2)}, u32[]{:S(2)}) collective-permute-start(bf16[1024,384]{1,0:T(8,128)(2,1)S(1)} %get-tuple-element.28.orr), channel_id=1, source_target_pairs={{0,2},{2,0},{4,6},{6,4},{8,10},{10,8},{12,14},{14,12},{16,18},{18,... | collective-permute-start | bytes 2359304 | tf_op jit(solution)/shard_map/ppermute | solution.py:176
  256.8 103.2 %collective-permute-start.26 = (bf16[384,1536]{1,0:T(8,128)(2,1)}, bf16[384,1536]{1,0:T(8,128)(2,1)}, u32[]{:S(2)}, u32[]{:S(2)}) collective-permute-start(bf16[384,1536]{1,0:T(8,128)(2,1)} %convolution_convert_fusion.6), channel_id=1, source_target_pairs={{0,2},{2,0},{4,6},{6,4},{8,10},{10,8},{12,14},{14,12},{16,18},{18,... | collective-permute-start | bytes 3538952 | tf_op jit(solution)/shard_map/ppermute | solution.py:176
  256.8 120.6 %collective-permute-start.21 = (bf16[384,1536]{1,0:T(8,128)(2,1)}, bf16[384,1536]{1,0:T(8,128)(2,1)}, u32[]{:S(2)}, u32[]{:S(2)}) collective-permute-start(bf16[384,1536]{1,0:T(8,128)(2,1)} %convolution_convert_fusion.8), channel_id=1, source_target_pairs={{0,2},{2,0},{4,6},{6,4},{8,10},{10,8},{12,14},{14,12},{16,18},{18,... | collective-permute-start | bytes 3538952 | tf_op jit(solution)/shard_map/ppermute | solution.py:176
  258.6 15.0 %collective-permute-start.14 = (bf16[384,384]{1,0:T(8,128)(2,1)}, bf16[384,384]{1,0:T(8,128)(2,1)}, u32[]{:S(2)}, u32[]{:S(2)}) collective-permute-start(bf16[384,384]{1,0:T(8,128)(2,1)} %convolution_convert_fusion.16), channel_id=1, source_target_pairs={{0,2},{2,0},{4,6},{6,4},{8,10},{10,8},{12,14},{14,12},{16,18},{18,... | collective-permute-start | bytes 884744 | tf_op jit(solution)/shard_map/ppermute | solution.py:176
  258.6 16.7 %collective-permute-start.15 = (bf16[384,384]{1,0:T(8,128)(2,1)}, bf16[384,384]{1,0:T(8,128)(2,1)}, u32[]{:S(2)}, u32[]{:S(2)}) collective-permute-start(bf16[384,384]{1,0:T(8,128)(2,1)} %convolution_convert_fusion.14), channel_id=1, source_target_pairs={{0,2},{2,0},{4,6},{6,4},{8,10},{10,8},{12,14},{14,12},{16,18},{18,... | collective-permute-start | bytes 884744 | tf_op jit(solution)/shard_map/ppermute | solution.py:176
  259.1 37.4 %collective-permute-start.5 = (bf16[1024,384]{1,0:T(8,128)(2,1)}, bf16[1024,384]{1,0:T(8,128)(2,1)}, u32[]{:S(2)}, u32[]{:S(2)}) collective-permute-start(bf16[1024,384]{1,0:T(8,128)(2,1)} %convolution_convert_fusion.12), channel_id=1, source_target_pairs={{0,2},{2,0},{4,6},{6,4},{8,10},{10,8},{12,14},{14,12},{16,18},{18,... | collective-permute-start | bytes 2359304 | tf_op jit(solution)/shard_map/ppermute | solution.py:176
  277.3 10.6 %collective-permute-start.16 = (bf16[384,384]{1,0:T(8,128)(2,1)S(1)}, bf16[384,384]{1,0:T(8,128)(2,1)S(1)}, u32[]{:S(2)}, u32[]{:S(2)}) collective-permute-start(bf16[384,384]{1,0:T(8,128)(2,1)S(1)} %get-tuple-element.171), channel_id=1, source_target_pairs={{0,1},{1,0},{2,3},{3,2},{4,5},{5,4},{6,7},{7,6},{8,9},{9,8},{10,11... | collective-permute-start | bytes 884744 | tf_op jit(solution)/shard_map/ppermute | solution.py:177
  294.4 59.8 %collective-permute-start.28 = (bf16[384,1536]{1,0:T(8,128)(2,1)}, bf16[384,1536]{1,0:T(8,128)(2,1)}, u32[]{:S(2)}, u32[]{:S(2)}) collective-permute-start(bf16[384,1536]{1,0:T(8,128)(2,1)} %convolution_convert_fusion.4), channel_id=1, source_target_pairs={{0,2},{2,0},{4,6},{6,4},{8,10},{10,8},{12,14},{14,12},{16,18},{18,... | collective-permute-start | bytes 3538952 | tf_op jit(solution)/shard_map/ppermute | solution.py:176
  294.4 86.7 %collective-permute-start.3 = (bf16[1024,768]{1,0:T(8,128)(2,1)}, bf16[1024,768]{1,0:T(8,128)(2,1)S(1)}, u32[]{:S(2)}, u32[]{:S(2)}) collective-permute-start(bf16[1024,768]{1,0:T(8,128)(2,1)} %fusion.23), channel_id=1, source_target_pairs={{0,0},{1,2},{2,1},{3,3},{4,4},{5,6},{6,5},{7,7},{8,8},{9,10},{10,9... | collective-permute-start | bytes 4718600 | tf_op jit(solution)/shard_map/ppermute | solution.py:466
  296.5 61.8 %collective-permute-start.18 = (bf16[96,384]{1,0:T(8,128)(2,1)S(1)}, bf16[96,384]{1,0:T(8,128)(2,1)S(1)}, u32[]{:S(2)}, u32[]{:S(2)}) collective-permute-start(bf16[96,384]{1,0:T(8,128)(2,1)S(1)} %slice.360), channel_id=1, source_target_pairs={{0,8},{2,10},{4,12},{6,14},{8,0},{10,2},{12,4},{14,6},{16,24},{18,... | collective-permute-start | bytes 221192 | tf_op jit(solution)/shard_map/ppermute | solution.py:176
  354.2 40.8 %collective-permute-start.6 = (bf16[1024,1152]{1,0:T(8,128)(2,1)S(1)}, bf16[1024,1152]{1,0:T(8,128)(2,1)S(1)}, u32[]{:S(2)}, u32[]{:S(2)}) collective-permute-start(bf16[1024,1152]{1,0:T(8,128)(2,1)S(1)} %copy-done.46), channel_id=1, source_target_pairs={{0,2},{2,0},{4,6},{6,4},{8,10},{10,8},{12,14},{14,12},{16,18},{18,... | collective-permute-start | bytes 7077896 | tf_op jit(solution)/shard_map/ppermute | solution.py:176
  358.4 16.1 %collective-permute-start.29 = (bf16[192,1536]{1,0:T(8,128)(2,1)S(1)}, bf16[192,1536]{1,0:T(8,128)(2,1)S(1)}, u32[]{:S(2)}, u32[]{:S(2)}) collective-permute-start(bf16[192,1536]{1,0:T(8,128)(2,1)S(1)} %slice.380), channel_id=1, source_target_pairs={{0,4},{2,6},{4,0},{6,2},{8,12},{10,14},{12,8},{14,10},{16,20},{18,... | collective-permute-start | bytes 1769480 | tf_op jit(solution)/shard_map/ppermute | solution.py:176
  360.0 16.2 %collective-permute-start.19 = (bf16[48,384]{1,0:T(8,128)(2,1)S(1)}, bf16[48,384]{1,0:T(8,128)(2,1)S(1)}, u32[]{:S(2)}, u32[]{:S(2)}) collective-permute-start(bf16[48,384]{1,0:T(8,128)(2,1)S(1)} %slice.362), channel_id=1, source_target_pairs={{0,16},{2,18},{4,20},{6,22},{8,24},{10,26},{12,28},{14,30},{16,0},... | collective-permute-start | bytes 110600 | tf_op jit(solution)/shard_map/ppermute | solution.py:176
  374.5 15.2 %collective-permute-start.27 = (bf16[192,1536]{1,0:T(8,128)(2,1)S(1)}, bf16[192,1536]{1,0:T(8,128)(2,1)S(1)}, u32[]{:S(2)}, u32[]{:S(2)}) collective-permute-start(bf16[192,1536]{1,0:T(8,128)(2,1)S(1)} %slice.378), channel_id=1, source_target_pairs={{0,4},{2,6},{4,0},{6,2},{8,12},{10,14},{12,8},{14,10},{16,20},{18,... | collective-permute-start | bytes 1769480 | tf_op jit(solution)/shard_map/ppermute | solution.py:176
  376.2 16.3 %collective-permute-start.30 = (bf16[192,1536]{1,0:T(8,128)(2,1)S(1)}, bf16[192,1536]{1,0:T(8,128)(2,1)S(1)}, u32[]{:S(2)}, u32[]{:S(2)}) collective-permute-start(bf16[192,1536]{1,0:T(8,128)(2,1)S(1)} %add_convert_fusion.16), channel_id=1, source_target_pairs={{0,1},{1,0},{2,3},{3,2},{4,5},{5,4},{6,7},{7,6},{8,9},{9,8},{10,11... | collective-permute-start | bytes 1769480 | tf_op jit(solution)/shard_map/ppermute | solution.py:177
  377.4 38.4 %collective-permute-start.20 = (bf16[384,1536]{1,0:T(8,128)(2,1)}, bf16[384,1536]{1,0:T(8,128)(2,1)}, u32[]{:S(2)}, u32[]{:S(2)}) collective-permute-start(bf16[384,1536]{1,0:T(8,128)(2,1)} %convolution_convert_fusion.10), channel_id=1, source_target_pairs={{0,2},{2,0},{4,6},{6,4},{8,10},{10,8},{12,14},{14,12},{16,18},{18,... | collective-permute-start | bytes 3538952 | tf_op jit(solution)/shard_map/ppermute | solution.py:176
  381.1 35.5 %collective-permute-start.22 = (bf16[384,1536]{1,0:T(8,128)(2,1)}, bf16[384,1536]{1,0:T(8,128)(2,1)}, u32[]{:S(2)}, u32[]{:S(2)}) collective-permute-start(bf16[384,1536]{1,0:T(8,128)(2,1)} %add_convert_fusion.9), channel_id=1, source_target_pairs={{0,1},{1,0},{2,3},{3,2},{4,5},{5,4},{6,7},{7,6},{8,9},{9,8},{10,11... | collective-permute-start | bytes 3538952 | tf_op jit(solution)/shard_map/ppermute | solution.py:177
  393.5 26.4 %collective-permute-start.31 = (bf16[96,1536]{1,0:T(8,128)(2,1)}, bf16[96,1536]{1,0:T(8,128)(2,1)}, u32[]{:S(2)}, u32[]{:S(2)}) collective-permute-start(bf16[96,1536]{1,0:T(8,128)(2,1)} %slice.382), channel_id=1, source_target_pairs={{0,8},{2,10},{4,12},{6,14},{8,0},{10,2},{12,4},{14,6},{16,24},{18,... | collective-permute-start | bytes 884744 | tf_op jit(solution)/shard_map/ppermute | solution.py:176
  415.3 9.2 %collective-permute-start.9 = (bf16[384,1280]{1,0:T(8,128)(2,1)S(1)}, bf16[384,1280]{1,0:T(8,128)(2,1)S(1)}, u32[]{:S(2)}, u32[]{:S(2)}) collective-permute-start(bf16[384,1280]{1,0:T(8,128)(2,1)S(1)} %get-tuple-element.147), channel_id=1, source_target_pairs={{0,2},{2,0},{4,6},{6,4},{8,10},{10,8},{12,14},{14,12},{16,18},{18,... | collective-permute-start | bytes 2949128 | tf_op jit(solution)/shard_map/ppermute | solution.py:176
  415.4 9.1 %collective-permute-start.8 = (bf16[384,1280]{1,0:T(8,128)(2,1)S(1)}, bf16[384,1280]{1,0:T(8,128)(2,1)S(1)}, u32[]{:S(2)}, u32[]{:S(2)}) collective-permute-start(bf16[384,1280]{1,0:T(8,128)(2,1)S(1)} %get-tuple-element.148), channel_id=1, source_target_pairs={{0,2},{2,0},{4,6},{6,4},{8,10},{10,8},{12,14},{14,12},{16,18},{18,... | collective-permute-start | bytes 2949128 | tf_op jit(solution)/shard_map/ppermute | solution.py:176
  419.3 14.3 %collective-permute-start.23 = (bf16[192,1536]{1,0:T(8,128)(2,1)S(1)}, bf16[192,1536]{1,0:T(8,128)(2,1)S(1)}, u32[]{:S(2)}, u32[]{:S(2)}) collective-permute-start(bf16[192,1536]{1,0:T(8,128)(2,1)S(1)} %slice.369), channel_id=1, source_target_pairs={{0,4},{2,6},{4,0},{6,2},{8,12},{10,14},{12,8},{14,10},{16,20},{18,... | collective-permute-start | bytes 1769480 | tf_op jit(solution)/shard_map/ppermute | solution.py:176
  421.0 8.6 %collective-permute-start.32 = (bf16[48,1536]{1,0:T(8,128)(2,1)S(1)}, bf16[48,1536]{1,0:T(8,128)(2,1)S(1)}, u32[]{:S(2)}, u32[]{:S(2)}) collective-permute-start(bf16[48,1536]{1,0:T(8,128)(2,1)S(1)} %slice.384), channel_id=1, source_target_pairs={{0,16},{2,18},{4,20},{6,22},{8,24},{10,26},{12,28},{14,30},{16,0},... | collective-permute-start | bytes 442376 | tf_op jit(solution)/shard_map/ppermute | solution.py:176
  425.0 22.3 %collective-permute-start.10 = (bf16[384,1280]{1,0:T(8,128)(2,1)S(1)}, bf16[384,1280]{1,0:T(8,128)(2,1)S(1)}, u32[]{:S(2)}, u32[]{:S(2)}) collective-permute-start(bf16[384,1280]{1,0:T(8,128)(2,1)S(1)} %broadcast_select_fusion), channel_id=1, source_target_pairs={{0,1},{1,0},{2,3},{3,2},{4,5},{5,4},{6,7},{7,6},{8,9},{9,8},{10,11... | collective-permute-start | bytes 2949128 | tf_op jit(solution)/shard_map/ppermute | solution.py:177
  433.9 26.1 %collective-permute-start.24 = (bf16[96,1536]{1,0:T(8,128)(2,1)S(1)}, bf16[96,1536]{1,0:T(8,128)(2,1)S(1)}, u32[]{:S(2)}, u32[]{:S(2)}) collective-permute-start(bf16[96,1536]{1,0:T(8,128)(2,1)S(1)} %slice.371), channel_id=1, source_target_pairs={{0,8},{2,10},{4,12},{6,14},{8,0},{10,2},{12,4},{14,6},{16,24},{18,... | collective-permute-start | bytes 884744 | tf_op jit(solution)/shard_map/ppermute | solution.py:176
  448.0 10.9 %collective-permute-start.11 = (bf16[192,1280]{1,0:T(8,128)(2,1)S(1)}, bf16[192,1280]{1,0:T(8,128)(2,1)S(1)}, u32[]{:S(2)}, u32[]{:S(2)}) collective-permute-start(bf16[192,1280]{1,0:T(8,128)(2,1)S(1)} %slice.346), channel_id=1, source_target_pairs={{0,4},{2,6},{4,0},{6,2},{8,12},{10,14},{12,8},{14,10},{16,20},{18,... | collective-permute-start | bytes 1474568 | tf_op jit(solution)/shard_map/ppermute | solution.py:176
  451.2 19.4 %collective-permute-start.7 = (bf16[1024,768]{1,0:T(8,128)(2,1)S(1)}, bf16[1024,768]{1,0:T(8,128)(2,1)S(1)}, u32[]{:S(2)}, u32[]{:S(2)}) collective-permute-start(bf16[1024,768]{1,0:T(8,128)(2,1)S(1)} %fusion.24), channel_id=1, source_target_pairs={{0,0},{1,2},{2,1},{3,3},{4,4},{5,6},{6,5},{7,7},{8,8},{9,10},{10,9... | collective-permute-start | bytes 4718600 | tf_op jit(solution)/shard_map/ppermute | solution.py:491
  459.1 7.4 %collective-permute-start.12 = (bf16[96,1280]{1,0:T(8,128)(2,1)S(1)}, bf16[96,1280]{1,0:T(8,128)(2,1)S(1)}, u32[]{:S(2)}, u32[]{:S(2)}) collective-permute-start(bf16[96,1280]{1,0:T(8,128)(2,1)S(1)} %slice.348), channel_id=1, source_target_pairs={{0,8},{2,10},{4,12},{6,14},{8,0},{10,2},{12,4},{14,6},{16,24},{18,... | collective-permute-start | bytes 737288 | tf_op jit(solution)/shard_map/ppermute | solution.py:176
  460.0 9.8 %collective-permute-start.25 = (bf16[48,1536]{1,0:T(8,128)(2,1)S(1)}, bf16[48,1536]{1,0:T(8,128)(2,1)S(1)}, u32[]{:S(2)}, u32[]{:S(2)}) collective-permute-start(bf16[48,1536]{1,0:T(8,128)(2,1)S(1)} %slice.373), channel_id=1, source_target_pairs={{0,16},{2,18},{4,20},{6,22},{8,24},{10,26},{12,28},{14,30},{16,0},... | collective-permute-start | bytes 442376 | tf_op jit(solution)/shard_map/ppermute | solution.py:176
  466.6 7.2 %collective-permute-start.13 = (bf16[48,1280]{1,0:T(8,128)(2,1)S(1)}, bf16[48,1280]{1,0:T(8,128)(2,1)S(1)}, u32[]{:S(2)}, u32[]{:S(2)}) collective-permute-start(bf16[48,1280]{1,0:T(8,128)(2,1)S(1)} %slice.350), channel_id=1, source_target_pairs={{0,16},{2,18},{4,20},{6,22},{8,24},{10,26},{12,28},{14,30},{16,0},... | collective-permute-start | bytes 368648 | tf_op jit(solution)/shard_map/ppermute | solution.py:176
  (59 other events, 881.9 us)
